TPU v7x, 128 devices: a whole 4x4x4 slice. The times are simulated.
128 devices in a mesh: ep: 4 (over x), tm: 32 (over y, z, core).
Axes of the slice: x: 4, y: 4, z: 4, core: 2. Of those that a mesh axis runs over, the one named last changes fastest.
Arguments:
- predictions: float32 [128, 1048576], P('ep', 'tm'), may hold values from -6 to 6
- leaf_index: int32 [128, 1048576], P('ep', 'tm'), may hold values from 0 to 63
- events: int32 [128, 1048576], P('ep', 'tm'), may hold values 0 or 1
- tie_start: int32 [1048576], P('tm'), may hold values from 0 to 1, as said below
Outputs:
- new_pred: float32 [128, 1048576], P('ep', 'tm')
- leaf_weights: float32 [128, 64], P('ep')
- grad_hess: bfloat16 [2, 128, 32, 32768], P(None, None, 'tm', 'ep')
Inputs may be any that keep to these rules, and one draw needn't show every extreme that they name: `tie_start`: every row whose index is a multiple of 128 begins a tie group.
All inputs are finite; a program needn't handle non-finite values. No bound on the sum of `events` on one device may be relied on, other than what follows from the above.
Results may differ from a plain program's by a relative error of at most 0.0023.
Values may be sent and summed in bfloat16 or wider, within the bound.
A program may use at most 128 MiB of HBM per device.

v0:
```python
import math

import jax
import jax.numpy as jnp
from jax import lax
from jax.experimental import pallas as pl
from jax.experimental.pallas import tpu as pltpu
from jax.sharding import PartitionSpec as P

LEAVES = 64
MESH = pl.DeviceIdType.MESH


def tm_combine(part, mode, cid):
    n = lax.axis_size("tm")
    rows = part.shape[0]

    def kernel(x_ref, out_ref, held, send_sem, recv_sem):
        me = lax.axis_index("tm")
        ep = lax.axis_index("ep")
        barrier = pltpu.get_barrier_semaphore()

        def greet(k, carry):
            p = lax.rem(me + k, n)
            pl.semaphore_signal(barrier, inc=1, device_id=(ep, p), device_id_type=MESH)
            return carry

        lax.fori_loop(1, n, greet, 0)
        pl.semaphore_wait(barrier, n - 1)

        def copy_to(p):
            return pltpu.make_async_remote_copy(
                src_ref=x_ref,
                dst_ref=held.at[me],
                send_sem=send_sem.at[p],
                recv_sem=recv_sem.at[me],
                device_id=(ep, p),
                device_id_type=MESH,
            )

        def copy_from(p):
            return pltpu.make_async_remote_copy(
                src_ref=x_ref,
                dst_ref=held.at[p],
                send_sem=send_sem.at[p],
                recv_sem=recv_sem.at[p],
                device_id=(ep, p),
                device_id_type=MESH,
            )

        def send(k, carry):
            copy_to(lax.rem(me + k, n)).start()
            return carry

        lax.fori_loop(1, n, send, 0)

        def wait(k, carry):
            p = lax.rem(me + k, n)
            copy_to(p).wait_send()
            copy_from(p).wait_recv()
            return carry

        lax.fori_loop(1, n, wait, 0)

        if mode == "all":
            total = x_ref[...]
        else:
            total = jnp.zeros((rows, 128), jnp.float32)

        def add(k, total):
            p = lax.rem(me + k, n)
            if mode == "all":
                keep = True
            elif mode == "later":
                keep = p > me
            else:
                keep = p < me
            return total + jnp.where(keep, held[p], 0.0)

        out_ref[...] = lax.fori_loop(1, n, add, total)

    return pl.pallas_call(
        kernel,
        out_shape=jax.ShapeDtypeStruct((rows, 128), jnp.float32),
        in_specs=[pl.BlockSpec(memory_space=pltpu.VMEM)],
        out_specs=pl.BlockSpec(memory_space=pltpu.VMEM),
        scratch_shapes=[
            pltpu.VMEM((n, rows, 128), jnp.float32),
            pltpu.SemaphoreType.DMA((n,)),
            pltpu.SemaphoreType.DMA((n,)),
        ],
        compiler_params=pltpu.CompilerParams(collective_id=cid, has_side_effects=True),
    )(part)


def exchange_and_sum(stacked, leaf_index, gradient, hessian, leaves, cid):
    m = lax.axis_size("ep")
    two, groups, length = stacked.shape
    width = length // m
    tiles = groups // 8
    side = leaves // 8
    chunk = math.gcd(length, 4096)
    cols_all = side * 4 * 8

    def histogram(leaf_ref, grad_ref, hess_ref, sums_ref):
        row_id = lax.broadcasted_iota(jnp.int32, (side * 8, cols_all), 0)
        col_id = lax.broadcasted_iota(jnp.int32, (side * 8, cols_all), 1)
        diagonal = lax.rem(row_id, 8) == lax.rem(col_id, 8)
        fold = (
            lax.broadcasted_iota(jnp.int32, (cols_all, side * 4), 0) // 8
            == lax.broadcasted_iota(jnp.int32, (cols_all, side * 4), 1)
        ).astype(jnp.float32)

        def one_tile(t, carry):
            rows = pl.ds(pl.multiple_of(t * 8, 8), 8)

            def one_chunk(step, total):
                cols = pl.ds(pl.multiple_of(step * chunk, chunk), chunk)
                leaf = leaf_ref[rows, cols]
                grad = grad_ref[rows, cols]
                hess = hess_ref[rows, cols]
                high = lax.shift_right_logical(leaf, 3)
                low = jnp.bitwise_and(leaf, 7)
                grad_hi = grad.astype(jnp.bfloat16).astype(jnp.float32)
                hess_hi = hess.astype(jnp.bfloat16).astype(jnp.float32)
                values = (grad_hi, grad - grad_hi, hess_hi, hess - hess_hi)
                ones = jnp.concatenate(
                    [jnp.where(high == a, 1.0, 0.0) for a in range(side)], axis=0
                ).astype(jnp.bfloat16)
                pieces = []
                for b in range(side):
                    hit = low == b
                    for value in values:
                        pieces.append(jnp.where(hit, value, 0.0))
                parts = jnp.concatenate(pieces, axis=0).astype(jnp.bfloat16)
                return total + lax.dot_general(
                    ones, parts, (((1,), (1,)), ((), ())), preferred_element_type=jnp.float32
                )

            total = jnp.zeros((side * 8, cols_all), jnp.float32)
            total = lax.fori_loop(0, length // chunk, one_chunk, total)
            total = jnp.where(diagonal, total, 0.0)
            sums_ref[t] = jnp.dot(
                total, fold, precision=lax.Precision.HIGHEST, preferred_element_type=jnp.float32
            )
            return carry

        lax.fori_loop(0, tiles, one_tile, 0)

    def kernel(src_ref, leaf_ref, grad_ref, hess_ref, out_ref, sums_ref, send_sem, recv_sem, local_sem):
        me = lax.axis_index("ep")
        tm = lax.axis_index("tm")
        barrier = pltpu.get_barrier_semaphore()
        for k in range(1, m):
            p = lax.rem(me + k, m)
            pl.semaphore_signal(barrier, inc=1, device_id=(p, tm), device_id_type=MESH)
        pl.semaphore_wait(barrier, m - 1)

        def copy_to(p):
            return pltpu.make_async_remote_copy(
                src_ref=src_ref.at[:, :, pl.ds(p * width, width)],
                dst_ref=out_ref.at[:, pl.ds(me * groups, groups), :],
                send_sem=send_sem.at[p],
                recv_sem=recv_sem.at[me],
                device_id=(p, tm),
                device_id_type=MESH,
            )

        def copy_from(p):
            return pltpu.make_async_remote_copy(
                src_ref=src_ref.at[:, :, pl.ds(me * width, width)],
                dst_ref=out_ref.at[:, pl.ds(p * groups, groups), :],
                send_sem=send_sem.at[p],
                recv_sem=recv_sem.at[p],
                device_id=(p, tm),
                device_id_type=MESH,
            )

        for k in range(1, m):
            copy_to(lax.rem(me + k, m)).start()
        local = pltpu.make_async_copy(
            src_ref.at[:, :, pl.ds(me * width, width)],
            out_ref.at[:, pl.ds(me * groups, groups), :],
            local_sem.at[0],
        )
        local.start()
        histogram(leaf_ref, grad_ref, hess_ref, sums_ref)
        local.wait()
        for k in range(1, m):
            p = lax.rem(me + k, m)
            copy_to(p).wait_send()
            copy_from(p).wait_recv()

    vmem = pl.BlockSpec(memory_space=pltpu.VMEM)
    grad_hess, sums = pl.pallas_call(
        kernel,
        out_shape=(
            jax.ShapeDtypeStruct((two, groups * m, width), stacked.dtype),
            jax.ShapeDtypeStruct((tiles, side * 8, side * 4), jnp.float32),
        ),
        in_specs=[pl.BlockSpec(memory_space=pl.ANY), vmem, vmem, vmem],
        out_specs=(pl.BlockSpec(memory_space=pl.ANY), vmem),
        scratch_shapes=[
            pltpu.SemaphoreType.DMA((m,)),
            pltpu.SemaphoreType.DMA((m,)),
            pltpu.SemaphoreType.DMA((1,)),
        ],
        compiler_params=pltpu.CompilerParams(collective_id=cid, has_side_effects=True),
    )(stacked, leaf_index, gradient, hessian)
    sums = sums.reshape(tiles, side, 8, side, 4).transpose(0, 2, 1, 3, 4)
    sums = sums.reshape(groups, leaves, 4)
    gsum = sums[:, :, 0] + sums[:, :, 1]
    hsum = sums[:, :, 2] + sums[:, :, 3]
    return grad_hess, jnp.stack([gsum, hsum], axis=1)


def lane_pad(vectors):
    width = vectors.shape[1]
    return jnp.pad(vectors, ((0, 0), (0, 128 - width)))


def tile_matrices(tie_start):
    length = tie_start.shape[0]
    blocks = length // 128
    starts = tie_start.reshape(blocks, 128)
    labels = jnp.arange(128, dtype=jnp.int32)
    first_local = lax.cummax(jnp.where(starts == 1, labels[None, :], 0), axis=1)
    next_start = jnp.concatenate([starts[:, 1:], jnp.ones((blocks, 1), jnp.int32)], axis=1)
    last_local = lax.cummin(jnp.where(next_start == 1, labels[None, :], 127), axis=1, reverse=True)
    backward = (labels[None, :, None] >= first_local[:, None, :]).astype(jnp.float32)
    forward = (labels[None, :, None] <= last_local[:, None, :]).astype(jnp.float32)
    return (backward, forward)


def block_cumsum(values, matrices, from_end):
    groups = values.shape[0]
    length = values.shape[1]
    blocks = length // 128
    shaped = values.reshape(groups, blocks, 128)
    within = jnp.einsum("ebj,bji->ebi", shaped, matrices, precision=lax.Precision.HIGHEST)
    totals = jnp.sum(shaped, axis=2)
    if from_end:
        offsets = jnp.cumsum(totals[:, ::-1], axis=1)[:, ::-1] - totals
    else:
        offsets = jnp.cumsum(totals, axis=1) - totals
    return (within + offsets[:, :, None]).reshape(groups, length)


def leaf_update(predictions, leaf_index, table):
    groups, length = leaf_index.shape
    tiles = groups // 8
    table = lane_pad(table)

    def kernel(table_ref, pred_ref, leaf_ref, out_ref):
        row = table_ref[...]

        def one(step, carry):
            cols = pl.ds(pl.multiple_of(step * 128, 128), 128)
            picked = jnp.take_along_axis(row, leaf_ref[:, cols], axis=1, mode="promise_in_bounds")
            out_ref[:, cols] = pred_ref[:, cols] + picked
            return carry

        lax.fori_loop(0, length // 128, one, 0, unroll=8)

    spec = pl.BlockSpec((8, length), lambda t: (t, 0))
    return pl.pallas_call(
        kernel,
        grid=(tiles,),
        out_shape=jax.ShapeDtypeStruct((groups, length), jnp.float32),
        in_specs=[pl.BlockSpec((8, 128), lambda t: (t, 0)), spec, spec],
        out_specs=spec,
    )(table, predictions, leaf_index)


def on_device(predictions, leaf_index, events, tie_start):
    groups = predictions.shape[0]
    length = predictions.shape[1]
    backward, forward = tile_matrices(tie_start)
    weight = jnp.exp(predictions)
    local_risk = block_cumsum(weight, backward, True)
    block_total = local_risk[:, 0]
    later_total = tm_combine(lane_pad(block_total[None, :]), "later", 0)[0, :groups]
    risk = local_risk + later_total[:, None]
    observed = events.astype(jnp.float32)
    inv_one = observed / risk
    inv_two = inv_one / risk
    local_one = block_cumsum(inv_one, forward, False)
    local_two = block_cumsum(inv_two, forward, False)
    pair = lane_pad(jnp.stack([local_one[:, -1], local_two[:, -1]]))
    earlier = tm_combine(pair, "earlier", 1)
    accum_one = local_one + earlier[0, :groups][:, None]
    accum_two = local_two + earlier[1, :groups][:, None]
    gradient = weight * accum_one - observed
    hessian = weight * accum_one - weight * weight * accum_two
    stacked = jnp.stack([gradient, hessian]).astype(jnp.bfloat16)
    grad_hess, partial_value = exchange_and_sum(stacked, leaf_index, gradient, hessian, LEAVES, 2)
    grad_hess = grad_hess.reshape(2, grad_hess.shape[1], 1, grad_hess.shape[2])
    totals = tm_combine(partial_value.reshape(groups, 2 * LEAVES), "all", 3)
    totals = totals.reshape(groups, 2, LEAVES)
    leaf_weights = -totals[:, 0] / (totals[:, 1] + 1.0)
    new_pred = leaf_update(predictions, leaf_index, leaf_weights)
    return (new_pred, leaf_weights, grad_hess)


def solution(mesh):
    placed = (P("ep", "tm"), P("ep", "tm"), P("ep", "tm"), P("tm"))
    return jax.shard_map(
        on_device,
        mesh=mesh,
        in_specs=placed,
        out_specs=(P("ep", "tm"), P("ep", None), P(None, None, "tm", "ep")),
        check_vma=False,
    )
```

profile of v0, /device:TPU:1, one launch (start us, length us, event | category | flops | bytes accessed | tf_op | source)
XLA Modules:
  0.0 198.4 jit_solution(9396974527813770415)
XLA Ops:
  0.6 4.7 %exponential_bitcast_fusion.1 = (f32[4,8,256,128]{3,1,2,0:T(8,128)S(1)}, f32[4,256,8,128]{3,2,1,0:T(8,128)}) fusion(f32[32,32768]{1,0:T(8,128)} %pred_ref.1), kind=kLoop, calls=%fused_computation.33 | loop fusion | bytes 12582912
  6.1 1.1 bitcast_reduce_fusion.2
  9.0 10.0 %fusion.14 = f32[256,4,8,128]{3,2,1,0:T(8,128)S(1)} fusion(f32[4,256,8,128]{3,2,1,0:T(8,128)} %get-tuple-element.27, s32[256,128]{1,0:T(8,128)S(1)} %copy.45, f32[32,256]{0,1:T(8,128)S(1)} %copy.49), kind=kOutput, calls=%fused_computation.26 | convolution fusion | flops 1615855616 | bytes 8552448 | tf_op jit(solution)/shard_map/ebj,bji->ebi/dot_general | solution.py:240
  19.3 1.7 copy-done.3
  21.7 13.5 %shard_map.67 = f32[1,128]{1,0:T(1,128)} custom-call(f32[1,128]{1,0:T(1,128)} %pad.13.x_ref), custom_call_target="tpu_custom_call" | custom-call | tf_op jit(solution)/shard_map/pallas_call | solution.py:82
  35.8 9.2 %fusion.24 = (f32[4,8,256,128]{3,1,2,0:T(8,128)S(1)}, f32[4,256,8,128]{3,2,1,0:T(8,128)}, f32[4,256,8,128]{3,2,1,0:T(8,128)}, f32[4,8,256,128]{3,1,2,0:T(8,128)}) fusion(f32[32]{0:T(128)S(1)} %slice_bitcast_fusion.2, f32[256,4,8,128]{3,2,1,0:T(8,128)} %copy-done.3, s32[32,32768]{1,0:T(8,128)} %param.6), kind=kLoop, calls=%fused_computation.65 | loop fusion | flops 5242880 | bytes 25165952
  45.8 1.1 bitcast_reduce_fusion.1
  48.3 4.4 %reduce_window_min.10 = s32[256,128]{0,1:T(8,128)S(1)} reduce-window(s32[256,128]{0,1:T(8,128)S(1)} %copy.42, s32[]{:T(128)} %constant.18.clone.1), window={size=1x128 pad=0_0x0_127}, to_apply=%region_0.1 | reduce-window | flops 4161536 | bytes 262148 | tf_op jit(solution)/shard_map/tile_matrices/reduce_window_min | solution.py:229
  52.8 10.0 %fusion.13 = f32[256,4,8,128]{3,2,1,0:T(8,128)S(1)} fusion(f32[4,256,8,128]{3,2,1,0:T(8,128)} %get-tuple-element.24, s32[256,128]{1,0:T(8,128)S(1)} %copy.43, f32[32,256]{0,1:T(8,128)S(1)} %copy.54), kind=kOutput, calls=%fused_computation.24 | convolution fusion | flops 1615855616 | bytes 8552448 | tf_op jit(solution)/shard_map/ebj,bji->ebi/dot_general | solution.py:240
  63.1 1.8 copy-done
  65.1 1.4 copy-done.1
  67.3 1.1 bitcast_reduce_fusion
  69.4 10.2 %fusion.12 = f32[256,4,8,128]{3,2,1,0:T(8,128)S(1)} fusion(f32[4,256,8,128]{3,2,1,0:T(8,128)} %get-tuple-element.23, s32[256,128]{1,0:T(8,128)S(1)} %copy.43, f32[32,256]{0,1:T(8,128)S(1)} %copy.59), kind=kOutput, calls=%fused_computation.22 | convolution fusion | flops 1615855616 | bytes 8552448 | tf_op jit(solution)/shard_map/ebj,bji->ebi/dot_general | solution.py:240
  79.9 1.7 copy-done.2
  82.4 10.2 %shard_map.68 = f32[2,128]{1,0:T(2,128)} custom-call(f32[2,128]{1,0:T(2,128)} %select_maximum_fusion.x_ref), custom_call_target="tpu_custom_call" | custom-call | tf_op jit(solution)/shard_map/pallas_call | solution.py:82
  92.6 0.8 slice_bitcast_fusion.1
  93.4 10.2 %convert_bitcast_fusion.1 = (bf16[1,32,32768]{2,1,0:T(8,128)(2,1)S(1)}, f32[32,32768]{1,0:T(8,128)}, bf16[1,32,32768]{2,1,0:T(8,128)(2,1)S(1)}, f32[32,32768]{1,0:T(8,128)}) fusion(s32[32,32768]{1,0:T(8,128)} %param.6, f32[32]{0:T(128)S(1)} %get-tuple-element.32, f32[256,4,8,128]{3,2,1,0:T(8,128)} %copy-done, f32[32,32768]{1,0:T(8,128)} %pred_ref.1, ...), kind=kLoop, calls=%fused_computation.35 | loop fusion | flops 10485760 | bytes 29360384 | tf_op jit(solution)/shard_map/stack | solution.py:295
  103.6 2.4 %pad_maximum_fusion.src_ref = bf16[2,32,32768]{2,1,0:T(8,128)(2,1)} fusion(bf16[1,32,32768]{2,1,0:T(8,128)(2,1)S(1)} %get-tuple-element.20, bf16[1,32,32768]{2,1,0:T(8,128)(2,1)S(1)} %get-tuple-element.16), kind=kLoop, calls=%fused_computation.20 | loop fusion | flops 2097152 | bytes 8388608 | tf_op jit(solution)/shard_map/stack | solution.py:295
  106.0 54.7 %shard_map.69 = (bf16[2,128,8192]{2,1,0:T(8,128)(2,1)}, f32[4,64,32]{2,1,0:T(8,128)}) custom-call(bf16[2,32,32768]{2,1,0:T(8,128)(2,1)} %pad_maximum_fusion.src_ref, s32[32,32768]{1,0:T(8,128)} %leaf_ref.3, f32[32,32768]{1,0:T(8,128)} %get-tuple-element.17.grad_ref, f32[32,32768]{1,0:T(8,128)} %get-tuple-element.21.hess_ref), custom_call_target="tpu_custom_call" | custom-call | tf_op jit(solution)/shard_map/pallas_call | solution.py:195
  160.7 1.0 copy.61
  163.2 14.8 %shard_map.70 = f32[32,128]{1,0:T(8,128)} custom-call(f32[32,128]{1,0:T(8,128)} %reshape.169.x_ref), custom_call_target="tpu_custom_call" | custom-call | tf_op jit(solution)/shard_map/pallas_call | solution.py:82
  178.1 0.8 reshape.170
  179.6 14.2 %shard_map.71 = f32[32,32768]{1,0:T(8,128)} custom-call(f32[32,128]{1,0:T(8,128)} %pad.15.table_ref, f32[32,32768]{1,0:T(8,128)} %pred_ref.1, s32[32,32768]{1,0:T(8,128)} %leaf_ref.3), custom_call_target="tpu_custom_call" | custom-call | tf_op jit(solution)/shard_map/pallas_call | solution.py:266
  193.7 4.6 %copy.136 = bf16[2,128,1,8192]{3,1,2,0:T(8,128)(2,1)} copy(bf16[2,128,1,8192]{3,1,2,0:T(8,128)(2,1)} %bitcast.147) | data formatting | bytes 8388608
  (62 shorter events, 11.6 us)
Async XLA Ops:
  6.1 2.5 %copy-start.4 = (s32[32768]{0:T(1024)S(1)}, s32[32768]{0:T(1024)}, u32[]{:S(2)}) copy-start(s32[32768]{0:T(1024)} %param.7) | copy-start | bytes 393220
  19.0 2.0 %copy-start.3 = (f32[256,4,8,128]{3,2,1,0:T(8,128)}, f32[256,4,8,128]{3,2,1,0:T(8,128)S(1)}, u32[]{:S(2)}) copy-start(f32[256,4,8,128]{3,2,1,0:T(8,128)S(1)} %fusion.14) | copy-start | bytes 12582916
  62.8 2.1 %copy-start = (f32[256,4,8,128]{3,2,1,0:T(8,128)}, f32[256,4,8,128]{3,2,1,0:T(8,128)S(1)}, u32[]{:S(2)}) copy-start(f32[256,4,8,128]{3,2,1,0:T(8,128)S(1)} %fusion.13) | copy-start | bytes 12582916
  62.8 3.7 %copy-start.1 = (f32[4,8,256,128]{3,1,2,0:T(8,128)S(1)}, f32[4,8,256,128]{3,1,2,0:T(8,128)}, u32[]{:S(2)}) copy-start(f32[4,8,256,128]{3,1,2,0:T(8,128)} %get-tuple-element.25) | copy-start | bytes 12582916
  79.6 2.0 %copy-start.2 = (f32[256,4,8,128]{3,2,1,0:T(8,128)}, f32[256,4,8,128]{3,2,1,0:T(8,128)S(1)}, u32[]{:S(2)}) copy-start(f32[256,4,8,128]{3,2,1,0:T(8,128)S(1)} %fusion.12) | copy-start | bytes 12582916
  179.0 14.8 %copy-start.5 = (f32[32,64]{1,0:T(8,128)}, f32[32,64]{1,0:T(8,128)S(1)}, u32[]{:S(2)}) copy-start(f32[32,64]{1,0:T(8,128)S(1)} %divide_bitcast_fusion) | copy-start | bytes 24580
where the time goes:
time: 199 us; the launch traced here: 198 us
  Pallas kernels  107 us (54%)
  other arithmetic  32.7 us (16%)
  matrix products  30.2 us (15%)
  local copies, waits for them, and re-layouts  27.1 us (14%)
    pallas_call x1, Pallas kernels, exchange_and_sum(): pl.pallas_call(kernel, out_shape=(jax.ShapeDtypeStruct((two, groups * m,...  54.7 us
    pallas_call x3, Pallas kernels, tm_combine(): pl.pallas_call(kernel, out_shape=jax.ShapeDtypeStruct((rows, 128), jnp.fl...  38.5 us
    dot_general x3, matrix products, block_cumsum(): jnp.einsum('ebj,bji->ebi', shaped, matrices, precision=lax.Precision.HIGH...  30.2 us
    unnamed x17, local copies, waits for them, and re-layouts  18.3 us
    pallas_call x1, Pallas kernels, leaf_update(): pl.pallas_call(kernel, grid=(tiles,), out_shape=jax.ShapeDtypeStruct((gro...  14.2 us
    another operation x2, other arithmetic, on_device(): stacked = jnp.stack([gradient, hessian]).astype(jnp.bfloat16)  12.6 us
    unnamed x1, other arithmetic  9.22 us
    another operation x1, other arithmetic, tile_matrices(): lax.cummin(jnp.where(next_start == 1, labels[None, :], 127), axis=1, reve...  4.39 us

commit v1 on v0

--- a/solution.py
+++ b/solution.py
@@ -214,6 +214,212 @@
     return grad_hess, jnp.stack([gsum, hsum], axis=1)
 
 
+def finish(stacked, leaf_index, gradient, hessian, predictions, leaves, cid):
+    m = lax.axis_size("ep")
+    n = lax.axis_size("tm")
+    two, groups, length = stacked.shape
+    width = length // m
+    tiles = groups // 8
+    side = leaves // 8
+    chunk = math.gcd(length, 4096)
+    cols_all = side * 4 * 8
+
+    def histogram(leaf_ref, grad_ref, hess_ref, mine):
+        row_id = lax.broadcasted_iota(jnp.int32, (side * 8, cols_all), 0)
+        col_id = lax.broadcasted_iota(jnp.int32, (side * 8, cols_all), 1)
+        diagonal = lax.rem(row_id, 8) == lax.rem(col_id, 8)
+        src = lax.broadcasted_iota(jnp.int32, (cols_all, 2 * leaves), 0)
+        dst = lax.broadcasted_iota(jnp.int32, (cols_all, 2 * leaves), 1)
+        src_b = src // 32
+        src_c = lax.rem(src // 8, 4)
+
+        def one_tile(t, carry):
+            rows = pl.ds(pl.multiple_of(t * 8, 8), 8)
+
+            def one_chunk(step, total):
+                cols = pl.ds(pl.multiple_of(step * chunk, chunk), chunk)
+                leaf = leaf_ref[rows, cols]
+                grad = grad_ref[rows, cols]
+                hess = hess_ref[rows, cols]
+                high = lax.shift_right_logical(leaf, 3)
+                low = jnp.bitwise_and(leaf, 7)
+                grad_hi = grad.astype(jnp.bfloat16).astype(jnp.float32)
+                hess_hi = hess.astype(jnp.bfloat16).astype(jnp.float32)
+                values = (grad_hi, grad - grad_hi, hess_hi, hess - hess_hi)
+                ones = jnp.concatenate(
+                    [jnp.where(high == a, 1.0, 0.0) for a in range(side)], axis=0
+                ).astype(jnp.bfloat16)
+                pieces = []
+                for b in range(side):
+                    hit = low == b
+                    for value in values:
+                        pieces.append(jnp.where(hit, value, 0.0))
+                parts = jnp.concatenate(pieces, axis=0).astype(jnp.bfloat16)
+                return total + lax.dot_general(
+                    ones, parts, (((1,), (1,)), ((), ())), preferred_element_type=jnp.float32
+                )
+
+            total = jnp.zeros((side * 8, cols_all), jnp.float32)
+            total = lax.fori_loop(0, length // chunk, one_chunk, total)
+            total = jnp.where(diagonal, total, 0.0)
+            out = jnp.zeros((8, 2 * leaves), jnp.float32)
+            for a in range(side):
+                fold = (dst == (src_c // 2) * leaves + a * side + src_b).astype(jnp.float32)
+                out = out + jnp.dot(
+                    total[a * 8:(a + 1) * 8, :], fold,
+                    precision=lax.Precision.HIGHEST, preferred_element_type=jnp.float32,
+                )
+            mine[rows, :] = out
+            return carry
+
+        lax.fori_loop(0, tiles, one_tile, 0)
+
+    def kernel(src_ref, leaf_ref, grad_ref, hess_ref, pred_ref,
+               out_ref, weights_ref, new_ref,
+               mine, held, ep_send, ep_recv, tm_send, tm_recv, local_sem):
+        me = lax.axis_index("ep")
+        tm = lax.axis_index("tm")
+        barrier = pltpu.get_barrier_semaphore()
+        for k in range(1, m):
+            p = lax.rem(me + k, m)
+            pl.semaphore_signal(barrier, inc=1, device_id=(p, tm), device_id_type=MESH)
+
+        def greet(k, carry):
+            p = lax.rem(tm + k, n)
+            pl.semaphore_signal(barrier, inc=1, device_id=(me, p), device_id_type=MESH)
+            return carry
+
+        lax.fori_loop(1, n, greet, 0)
+        pl.semaphore_wait(barrier, (m - 1) + (n - 1))
+
+        def ep_to(p):
+            return pltpu.make_async_remote_copy(
+                src_ref=src_ref.at[:, :, pl.ds(p * width, width)],
+                dst_ref=out_ref.at[:, pl.ds(me * groups, groups), :],
+                send_sem=ep_send.at[p],
+                recv_sem=ep_recv.at[me],
+                device_id=(p, tm),
+                device_id_type=MESH,
+            )
+
+        def ep_from(p):
+            return pltpu.make_async_remote_copy(
+                src_ref=src_ref.at[:, :, pl.ds(me * width, width)],
+                dst_ref=out_ref.at[:, pl.ds(p * groups, groups), :],
+                send_sem=ep_send.at[p],
+                recv_sem=ep_recv.at[p],
+                device_id=(p, tm),
+                device_id_type=MESH,
+            )
+
+        for k in range(1, m):
+            ep_to(lax.rem(me + k, m)).start()
+        local = pltpu.make_async_copy(
+            src_ref.at[:, :, pl.ds(me * width, width)],
+            out_ref.at[:, pl.ds(me * groups, groups), :],
+            local_sem.at[0],
+        )
+        local.start()
+
+        histogram(leaf_ref, grad_ref, hess_ref, mine)
+        staged = pltpu.make_async_copy(mine, held.at[tm], local_sem.at[1])
+        staged.start()
+        staged.wait()
+
+        def tm_to(p):
+            return pltpu.make_async_remote_copy(
+                src_ref=held.at[tm],
+                dst_ref=held.at[tm],
+                send_sem=tm_send.at[p],
+                recv_sem=tm_recv.at[tm],
+                device_id=(me, p),
+                device_id_type=MESH,
+            )
+
+        def tm_from(p):
+            return pltpu.make_async_remote_copy(
+                src_ref=held.at[tm],
+                dst_ref=held.at[p],
+                send_sem=tm_send.at[p],
+                recv_sem=tm_recv.at[p],
+                device_id=(me, p),
+                device_id_type=MESH,
+            )
+
+        def send(k, carry):
+            tm_to(lax.rem(tm + k, n)).start()
+            return carry
+
+        lax.fori_loop(1, n, send, 0)
+
+        def wait(k, carry):
+            p = lax.rem(tm + k, n)
+            tm_to(p).wait_send()
+            tm_from(p).wait_recv()
+            return carry
+
+        lax.fori_loop(1, n, wait, 0)
+
+        def add(k, total):
+            return total + held[lax.rem(tm + k, n)]
+
+        totals = lax.fori_loop(1, n, add, held[tm])
+        lane = lax.broadcasted_iota(jnp.int32, (groups, 2 * leaves), 1)
+        hsum = pltpu.roll(totals, leaves, 1)
+        table = jnp.where(lane < leaves, -totals / (hsum + 1.0), 0.0)
+        weights_ref[...] = table[:, :leaves]
+
+        mine[...] = table
+
+        def one_tile(t, carry):
+            rows = pl.ds(pl.multiple_of(t * 8, 8), 8)
+            row = mine[rows, :]
+
+            def one(step, carry):
+                cols = pl.ds(pl.multiple_of(step * 128, 128), 128)
+                picked = jnp.take_along_axis(
+                    row, leaf_ref[rows, cols], axis=1, mode="promise_in_bounds"
+                )
+                new_ref[rows, cols] = pred_ref[rows, cols] + picked
+                return carry
+
+            lax.fori_loop(0, length // 128, one, 0, unroll=8)
+            return carry
+
+        lax.fori_loop(0, tiles, one_tile, 0)
+
+        local.wait()
+        for k in range(1, m):
+            p = lax.rem(me + k, m)
+            ep_to(p).wait_send()
+            ep_from(p).wait_recv()
+
+    vmem = pl.BlockSpec(memory_space=pltpu.VMEM)
+    grad_hess, leaf_weights, new_pred = pl.pallas_call(
+        kernel,
+        out_shape=(
+            jax.ShapeDtypeStruct((two, groups * m, width), stacked.dtype),
+            jax.ShapeDtypeStruct((groups, leaves), jnp.float32),
+            jax.ShapeDtypeStruct((groups, length), jnp.float32),
+        ),
+        in_specs=[pl.BlockSpec(memory_space=pl.ANY), vmem, vmem, vmem, vmem],
+        out_specs=(pl.BlockSpec(memory_space=pl.ANY), vmem, vmem),
+        scratch_shapes=[
+            pltpu.VMEM((groups, 2 * leaves), jnp.float32),
+            pltpu.VMEM((n, groups, 2 * leaves), jnp.float32),
+            pltpu.SemaphoreType.DMA((m,)),
+            pltpu.SemaphoreType.DMA((m,)),
+            pltpu.SemaphoreType.DMA((n,)),
+            pltpu.SemaphoreType.DMA((n,)),
+            pltpu.SemaphoreType.DMA((2,)),
+        ],
+        compiler_params=pltpu.CompilerParams(
+            collective_id=cid, has_side_effects=True, vmem_limit_bytes=60 * 1024 * 1024
+        ),
+    )(stacked, leaf_index, gradient, hessian, predictions)
+    return grad_hess, leaf_weights, new_pred
+
+
 def lane_pad(vectors):
     width = vectors.shape[1]
     return jnp.pad(vectors, ((0, 0), (0, 128 - width)))
@@ -293,12 +499,10 @@
     gradient = weight * accum_one - observed
     hessian = weight * accum_one - weight * weight * accum_two
     stacked = jnp.stack([gradient, hessian]).astype(jnp.bfloat16)
-    grad_hess, partial_value = exchange_and_sum(stacked, leaf_index, gradient, hessian, LEAVES, 2)
+    grad_hess, leaf_weights, new_pred = finish(
+        stacked, leaf_index, gradient, hessian, predictions, LEAVES, 2
+    )
     grad_hess = grad_hess.reshape(2, grad_hess.shape[1], 1, grad_hess.shape[2])
-    totals = tm_combine(partial_value.reshape(groups, 2 * LEAVES), "all", 3)
-    totals = totals.reshape(groups, 2, LEAVES)
-    leaf_weights = -totals[:, 0] / (totals[:, 1] + 1.0)
-    new_pred = leaf_update(predictions, leaf_index, leaf_weights)
     return (new_pred, leaf_weights, grad_hess)
 
 

time: 199 us -> 175 us (0.88)
  Pallas kernels: 107 us -> 84.8 us
    pallas_call x3 -> x2, Pallas kernels: 38.5 us -> 23.7 us  [tm_combine(): pl.pallas_call(kernel, out_shape=jax.ShapeDtypeStruct((rows, 128), jnp.fl...]
    pallas_call x2 -> x1, Pallas kernels: 68.9 us -> 61.1 us  [finish(): pl.pallas_call(kernel, out_shape=(jax.ShapeDtypeStruct((two, groups * m,...]
    unnamed x17 -> x21, local copies, waits for them, and re-layouts: 18.3 us -> 20.9 us
where the time goes in v1:
time: 175 us; the launch traced here: 174 us
  Pallas kernels  84.8 us (48%)
  other arithmetic  32.7 us (19%)
  matrix products  30.2 us (17%)
  local copies, waits for them, and re-layouts  25.8 us (15%)
    pallas_call x1, Pallas kernels, finish(): pl.pallas_call(kernel, out_shape=(jax.ShapeDtypeStruct((two, groups * m,...  61.1 us
    dot_general x3, matrix products, block_cumsum(): jnp.einsum('ebj,bji->ebi', shaped, matrices, precision=lax.Precision.HIGH...  30.2 us
    pallas_call x2, Pallas kernels, tm_combine(): pl.pallas_call(kernel, out_shape=jax.ShapeDtypeStruct((rows, 128), jnp.fl...  23.7 us
    unnamed x21, local copies, waits for them, and re-layouts  20.9 us
    another operation x2, other arithmetic, on_device(): stacked = jnp.stack([gradient, hessian]).astype(jnp.bfloat16)  12.5 us
    unnamed x1, other arithmetic  9.22 us
    another operation x1, other arithmetic, tile_matrices(): lax.cummin(jnp.where(next_start == 1, labels[None, :], 127), axis=1, reve...  4.39 us

profile of v1, /device:TPU:1, one launch (start us, length us, event | category | flops | bytes accessed | tf_op | source)
XLA Modules:
  0.0 174.3 jit_solution(17227977805357607239)
XLA Ops:
  0.6 4.7 %exponential_bitcast_fusion.1 = (f32[4,8,256,128]{3,1,2,0:T(8,128)S(1)}, f32[4,256,8,128]{3,2,1,0:T(8,128)}) fusion(f32[32,32768]{1,0:T(8,128)} %pred_ref.1), kind=kLoop, calls=%fused_computation.33 | loop fusion | bytes 12582912
  5.4 0.7 copy.48
  6.1 1.1 bitcast_reduce_fusion.2
  9.0 10.0 %fusion.14 = f32[256,4,8,128]{3,2,1,0:T(8,128)S(1)} fusion(f32[4,256,8,128]{3,2,1,0:T(8,128)} %get-tuple-element.26, s32[256,128]{1,0:T(8,128)S(1)} %copy.19, f32[32,256]{0,1:T(8,128)S(1)} %copy.23), kind=kOutput, calls=%fused_computation.26 | convolution fusion | flops 1615855616 | bytes 8552448 | tf_op jit(solution)/shard_map/ebj,bji->ebi/dot_general | solution.py:446
  19.3 1.7 copy-done.3
  21.7 13.5 %shard_map.67 = f32[1,128]{1,0:T(1,128)} custom-call(f32[1,128]{1,0:T(1,128)} %pad.9.x_ref), custom_call_target="tpu_custom_call" | custom-call | tf_op jit(solution)/shard_map/pallas_call | solution.py:82
  35.8 9.2 %fusion.22 = (f32[4,8,256,128]{3,1,2,0:T(8,128)S(1)}, f32[4,256,8,128]{3,2,1,0:T(8,128)}, f32[4,256,8,128]{3,2,1,0:T(8,128)}, f32[4,8,256,128]{3,1,2,0:T(8,128)}) fusion(f32[32]{0:T(128)S(1)} %slice_bitcast_fusion.2, f32[256,4,8,128]{3,2,1,0:T(8,128)} %copy-done.3, s32[32,32768]{1,0:T(8,128)} %param.6), kind=kLoop, calls=%fused_computation.59 | loop fusion | flops 5242880 | bytes 25165952
  45.0 0.7 copy.49
  45.8 1.1 bitcast_reduce_fusion.1
  47.0 0.8 reduce-window.24
  48.3 4.4 %reduce_window_min.10 = s32[256,128]{0,1:T(8,128)S(1)} reduce-window(s32[256,128]{0,1:T(8,128)S(1)} %copy.16, s32[]{:T(128)} %constant.17.clone.1), window={size=1x128 pad=0_0x0_127}, to_apply=%region_0.1 | reduce-window | flops 4161536 | bytes 262148 | tf_op jit(solution)/shard_map/tile_matrices/reduce_window_min | solution.py:435
  52.8 10.0 %fusion.13 = f32[256,4,8,128]{3,2,1,0:T(8,128)S(1)} fusion(f32[4,256,8,128]{3,2,1,0:T(8,128)} %get-tuple-element.23, s32[256,128]{1,0:T(8,128)S(1)} %copy.17, f32[32,256]{0,1:T(8,128)S(1)} %copy.28), kind=kOutput, calls=%fused_computation.24 | convolution fusion | flops 1615855616 | bytes 8552448 | tf_op jit(solution)/shard_map/ebj,bji->ebi/dot_general | solution.py:446
  63.1 1.8 %copy-done = f32[256,4,8,128]{3,2,1,0:T(8,128)} copy-done((f32[256,4,8,128]{3,2,1,0:T(8,128)}, f32[256,4,8,128]{3,2,1,0:T(8,128)S(1)}, u32[]{:S(2)}) %copy-start) | copy-done | bytes 4194328
  65.1 1.4 copy-done.1
  67.3 1.1 bitcast_reduce_fusion
  69.4 10.2 %fusion.12 = f32[256,4,8,128]{3,2,1,0:T(8,128)S(1)} fusion(f32[4,256,8,128]{3,2,1,0:T(8,128)} %get-tuple-element.22, s32[256,128]{1,0:T(8,128)S(1)} %copy.17, f32[32,256]{0,1:T(8,128)S(1)} %copy.33), kind=kOutput, calls=%fused_computation.22 | convolution fusion | flops 1615855616 | bytes 8552448 | tf_op jit(solution)/shard_map/ebj,bji->ebi/dot_general | solution.py:446
  79.9 1.7 copy-done.2
  82.4 10.2 %shard_map.68 = f32[2,128]{1,0:T(2,128)} custom-call(f32[2,128]{1,0:T(2,128)} %select_maximum_fusion.x_ref), custom_call_target="tpu_custom_call" | custom-call | tf_op jit(solution)/shard_map/pallas_call | solution.py:82
  92.6 0.8 slice_bitcast_fusion.1
  93.4 10.2 %convert_bitcast_fusion.1 = (bf16[1,32,32768]{2,1,0:T(8,128)(2,1)S(1)}, f32[32,32768]{1,0:T(8,128)}, bf16[1,32,32768]{2,1,0:T(8,128)(2,1)S(1)}, f32[32,32768]{1,0:T(8,128)}) fusion(s32[32,32768]{1,0:T(8,128)} %param.6, f32[32]{0:T(128)S(1)} %get-tuple-element.27, f32[256,4,8,128]{3,2,1,0:T(8,128)} %copy-done, f32[32,32768]{1,0:T(8,128)} %pred_ref.1, ...), kind=kLoop, calls=%fused_computation.35 | loop fusion | flops 10485760 | bytes 29360384 | tf_op jit(solution)/shard_map/stack | solution.py:501
  103.5 2.4 %pad_maximum_fusion.src_ref = bf16[2,32,32768]{2,1,0:T(8,128)(2,1)} fusion(bf16[1,32,32768]{2,1,0:T(8,128)(2,1)S(1)} %get-tuple-element.19, bf16[1,32,32768]{2,1,0:T(8,128)(2,1)S(1)} %get-tuple-element.15), kind=kLoop, calls=%fused_computation.20 | loop fusion | flops 2097152 | bytes 8388608 | tf_op jit(solution)/shard_map/stack | solution.py:501
  105.9 61.1 %shard_map.69 = (bf16[2,128,8192]{2,1,0:T(8,128)(2,1)}, f32[32,64]{1,0:T(8,128)}, f32[32,32768]{1,0:T(8,128)}) custom-call(bf16[2,32,32768]{2,1,0:T(8,128)(2,1)} %pad_maximum_fusion.src_ref, s32[32,32768]{1,0:T(8,128)} %leaf_ref.1, f32[32,32768]{1,0:T(8,128)} %get-tuple-element.16.grad_ref, f32[32,32768]{1,0:T(8,128)} %get-tuple-element.20.hess_ref, ...), custom_call_target="tpu_custom_call" | custom-call | tf_op jit(solution)/shard_map/pallas_call | solution.py:398
  167.1 4.6 %copy.105 = f32[32,32768]{1,0:T(8,128)} copy(f32[32,32768]{1,0:T(8,128)} %get-tuple-element.32) | data formatting | bytes 8388608
  172.3 2.0 %copy.107 = bf16[2,128,1,8192]{3,1,2,0:T(8,128)(2,1)} copy(bf16[2,128,1,8192]{3,1,2,0:T(8,128)(2,1)S(1)} %bitcast.132) | data formatting | bytes 8388608
  (52 shorter events, 7.8 us)
Async XLA Ops:
  6.1 2.5 %copy-start.5 = (s32[32768]{0:T(1024)S(1)}, s32[32768]{0:T(1024)}, u32[]{:S(2)}) copy-start(s32[32768]{0:T(1024)} %param.7) | copy-start | bytes 393220
  19.0 2.0 %copy-start.3 = (f32[256,4,8,128]{3,2,1,0:T(8,128)}, f32[256,4,8,128]{3,2,1,0:T(8,128)S(1)}, u32[]{:S(2)}) copy-start(f32[256,4,8,128]{3,2,1,0:T(8,128)S(1)} %fusion.14) | copy-start | bytes 12582916
  62.8 2.1 %copy-start = (f32[256,4,8,128]{3,2,1,0:T(8,128)}, f32[256,4,8,128]{3,2,1,0:T(8,128)S(1)}, u32[]{:S(2)}) copy-start(f32[256,4,8,128]{3,2,1,0:T(8,128)S(1)} %fusion.13) | copy-start | bytes 12582916
  62.8 3.7 %copy-start.1 = (f32[4,8,256,128]{3,1,2,0:T(8,128)S(1)}, f32[4,8,256,128]{3,1,2,0:T(8,128)}, u32[]{:S(2)}) copy-start(f32[4,8,256,128]{3,1,2,0:T(8,128)} %get-tuple-element.24) | copy-start | bytes 12582916
  79.6 2.0 %copy-start.2 = (f32[256,4,8,128]{3,2,1,0:T(8,128)}, f32[256,4,8,128]{3,2,1,0:T(8,128)S(1)}, u32[]{:S(2)}) copy-start(f32[256,4,8,128]{3,2,1,0:T(8,128)S(1)} %fusion.12) | copy-start | bytes 12582916
  167.1 4.6 %copy-start.6 = (f32[32,64]{1,0:T(8,128)S(1)}, f32[32,64]{1,0:T(8,128)}, u32[]{:S(2)}) copy-start(f32[32,64]{1,0:T(8,128)} %get-tuple-element.33) | copy-start | bytes 24580
  167.1 5.2 %copy-start.4 = (bf16[2,128,8192]{2,1,0:T(8,128)(2,1)S(1)}, bf16[2,128,8192]{2,1,0:T(8,128)(2,1)}, u32[]{:S(2)}) copy-start(bf16[2,128,8192]{2,1,0:T(8,128)(2,1)} %get-tuple-element.8) | copy-start | bytes 12582916

commit v2 on v1

--- a/solution.py
+++ b/solution.py
@@ -443,7 +443,7 @@
     length = values.shape[1]
     blocks = length // 128
     shaped = values.reshape(groups, blocks, 128)
-    within = jnp.einsum("ebj,bji->ebi", shaped, matrices, precision=lax.Precision.HIGHEST)
+    within = jnp.einsum("ebj,bji->ebi", shaped, matrices, precision=lax.Precision.HIGH)
     totals = jnp.sum(shaped, axis=2)
     if from_end:
         offsets = jnp.cumsum(totals[:, ::-1], axis=1)[:, ::-1] - totals
@@ -490,8 +490,9 @@
     observed = events.astype(jnp.float32)
     inv_one = observed / risk
     inv_two = inv_one / risk
-    local_one = block_cumsum(inv_one, forward, False)
-    local_two = block_cumsum(inv_two, forward, False)
+    local_both = block_cumsum(jnp.concatenate([inv_one, inv_two]), forward, False)
+    local_one = local_both[:groups]
+    local_two = local_both[groups:]
     pair = lane_pad(jnp.stack([local_one[:, -1], local_two[:, -1]]))
     earlier = tm_combine(pair, "earlier", 1)
     accum_one = local_one + earlier[0, :groups][:, None]

time: 175 us -> 171 us (0.977)
  matrix products: 30.2 us -> 15.5 us
  other arithmetic: 32.7 us -> 41.8 us
  local copies, waits for them, and re-layouts: 25.8 us -> 28.1 us
    dot_general x3 -> x2, matrix products: 30.2 us -> 15.5 us  [block_cumsum(): jnp.einsum('ebj,bji->ebi', shaped, matrices, precision=lax.Precision.HIGH)]
    div x0 -> x1, other arithmetic: none -> 7.92 us  [on_device(): inv_one = observed / risk]
    unnamed x21 -> x19, local copies, waits for them, and re-layouts: 20.9 us -> 23.4 us
    unnamed x1, other arithmetic: 9.22 us -> 11.2 us
where the time goes in v2:
time: 171 us
  Pallas kernels  84.8 us (50%)
  other arithmetic  41.8 us (24%)
  local copies, waits for them, and re-layouts  28.1 us (16%)
  matrix products  15.5 us (9%)
    pallas_call x1, Pallas kernels, finish(): pl.pallas_call(kernel, out_shape=(jax.ShapeDtypeStruct((two, groups * m,...  61.1 us
    pallas_call x2, Pallas kernels, tm_combine(): pl.pallas_call(kernel, out_shape=jax.ShapeDtypeStruct((rows, 128), jnp.fl...  23.7 us
    unnamed x19, local copies, waits for them, and re-layouts  23.4 us
    dot_general x2, matrix products, block_cumsum(): jnp.einsum('ebj,bji->ebi', shaped, matrices, precision=lax.Precision.HIGH)  15.5 us
    another operation x2, other arithmetic, on_device(): stacked = jnp.stack([gradient, hessian]).astype(jnp.bfloat16)  12.5 us
    unnamed x1, other arithmetic  11.2 us
    div x1, other arithmetic, on_device(): inv_one = observed / risk  7.92 us
    another operation x1, other arithmetic, tile_matrices(): lax.cummin(jnp.where(next_start == 1, labels[None, :], 127), axis=1, reve...  4.39 us

profile of v2, /device:TPU:1, one launch (start us, length us, event | category | flops | bytes accessed | tf_op | source)
XLA Modules:
  0.0 171.2 jit_solution(5871385925486278817)
XLA Ops:
  0.6 4.7 %exponential_bitcast_fusion.1 = (f32[4,8,256,128]{3,1,2,0:T(8,128)S(1)}, f32[4,256,8,128]{3,2,1,0:T(8,128)}) fusion(f32[32,32768]{1,0:T(8,128)} %pred_ref.1), kind=kLoop, calls=%fused_computation.30 | loop fusion | bytes 12582912
  5.4 0.7 copy.40
  6.1 1.1 bitcast_reduce_fusion.1
  9.2 7.3 %fusion.10 = f32[256,4,8,128]{3,2,1,0:T(8,128)S(1)} fusion(f32[4,256,8,128]{3,2,1,0:T(8,128)} %get-tuple-element.28, s32[256,128]{1,0:T(8,128)S(1)} %copy.18, f32[32,256]{0,1:T(8,128)S(1)} %copy.22), kind=kOutput, calls=%fused_computation.23 | convolution fusion | flops 810549248 | bytes 8552448 | tf_op jit(solution)/shard_map/ebj,bji->ebi/dot_general | solution.py:446
  16.8 1.7 %copy-done.2 = f32[256,4,8,128]{3,2,1,0:T(8,128)} copy-done((f32[256,4,8,128]{3,2,1,0:T(8,128)}, f32[256,4,8,128]{3,2,1,0:T(8,128)S(1)}, u32[]{:S(2)}) %copy-start.2) | copy-done | bytes 4194328
  19.2 13.5 %shard_map.67 = f32[1,128]{1,0:T(1,128)} custom-call(f32[1,128]{1,0:T(1,128)} %pad.9.x_ref), custom_call_target="tpu_custom_call" | custom-call | tf_op jit(solution)/shard_map/pallas_call | solution.py:82
  32.7 0.7 slice_bitcast_fusion.4
  33.3 7.9 %convert_divide_fusion = (f32[32,32768]{1,0:T(8,128)}, f32[32,32768]{1,0:T(8,128)}) fusion(s32[32,32768]{1,0:T(8,128)} %param.6, f32[32]{0:T(128)S(1)} %slice_bitcast_fusion.4, f32[256,4,8,128]{3,2,1,0:T(8,128)} %copy-done.2), kind=kLoop, calls=%fused_computation.28 | loop fusion | flops 5242880 | bytes 16777344 | tf_op jit(solution)/shard_map/div | solution.py:491
  41.3 11.2 %fusion.6 = (f32[8,256,8,128]{3,2,1,0:T(8,128)}, f32[8,8,256,128]{3,1,2,0:T(8,128)}) fusion(f32[32,32768]{1,0:T(8,128)} %get-tuple-element.22, f32[32,32768]{1,0:T(8,128)} %get-tuple-element.21), kind=kLoop, calls=%fused_computation.11 | loop fusion | flops 2097152 | bytes 25165824
  52.5 4.9 %copy.41 = f32[8,8,256,128]{3,2,1,0:T(8,128)S(1)} copy(f32[8,8,256,128]{3,1,2,0:T(8,128)} %get-tuple-element.26) | data formatting | bytes 16777216
  57.3 2.2 %bitcast_reduce_fusion = f32[64,256]{1,0:T(8,128)S(1)} fusion(f32[8,8,256,128]{3,2,1,0:T(8,128)S(1)} %copy.41), kind=kLoop, calls=%fused_computation.4 | loop fusion | flops 2080768 | bytes 8454144 | tf_op jit(solution)/shard_map/reduce_sum | solution.py:447
  59.6 0.8 reduce-window.16
  61.0 4.4 %reduce_window_min.10 = s32[256,128]{0,1:T(8,128)S(1)} reduce-window(s32[256,128]{0,1:T(8,128)S(1)} %copy.15, s32[]{:T(128)} %constant.18.clone.1), window={size=1x128 pad=0_0x0_127}, to_apply=%region_0.1 | reduce-window | flops 4161536 | bytes 262148 | tf_op jit(solution)/shard_map/tile_matrices/reduce_window_min | solution.py:435
  65.5 8.2 %bitcast_add_fusion = f32[64,256,128]{2,0,1:T(8,128)S(1)} fusion(f32[64,256]{0,1:T(8,128)S(1)} %copy.27, f32[8,256,8,128]{3,2,1,0:T(8,128)} %get-tuple-element.25, s32[256,128]{1,0:T(8,128)S(1)} %copy.16), kind=kOutput, calls=%fused_computation.8 | convolution fusion | flops 1616904192 | bytes 16973824 | tf_op jit(solution)/shard_map/ebj,bji->ebi/dot_general | solution.py:446
  73.7 1.2 slice_bitcast_fusion.1
  75.5 1.4 copy-done
  77.0 1.4 copy-done.1
  79.3 10.2 %shard_map.68 = f32[2,128]{1,0:T(2,128)} custom-call(f32[2,128]{1,0:T(2,128)} %select_maximum_fusion.x_ref), custom_call_target="tpu_custom_call" | custom-call | tf_op jit(solution)/shard_map/pallas_call | solution.py:82
  89.5 0.8 slice_bitcast_fusion.3
  90.2 10.2 %convert_bitcast_fusion.1 = (bf16[1,32,32768]{2,1,0:T(8,128)(2,1)S(1)}, f32[32,32768]{1,0:T(8,128)}, bf16[1,32,32768]{2,1,0:T(8,128)(2,1)S(1)}, f32[32,32768]{1,0:T(8,128)}) fusion(s32[32,32768]{1,0:T(8,128)} %param.6, f32[32]{0:T(128)S(1)} %get-tuple-element.29, f32[256,4,8,128]{3,2,1,0:T(8,128)} %copy-done, f32[32,32768]{1,0:T(8,128)} %pred_ref.1, ...), kind=kLoop, calls=%fused_computation.32 | loop fusion | flops 10485760 | bytes 29360384 | tf_op jit(solution)/shard_map/stack | solution.py:502
  100.4 2.4 %pad_maximum_fusion.1.src_ref = bf16[2,32,32768]{2,1,0:T(8,128)(2,1)} fusion(bf16[1,32,32768]{2,1,0:T(8,128)(2,1)S(1)} %get-tuple-element.19, bf16[1,32,32768]{2,1,0:T(8,128)(2,1)S(1)} %get-tuple-element.15), kind=kLoop, calls=%fused_computation.21 | loop fusion | flops 2097152 | bytes 8388608 | tf_op jit(solution)/shard_map/stack | solution.py:502
  102.8 61.1 %shard_map.69 = (bf16[2,128,8192]{2,1,0:T(8,128)(2,1)}, f32[32,64]{1,0:T(8,128)}, f32[32,32768]{1,0:T(8,128)}) custom-call(bf16[2,32,32768]{2,1,0:T(8,128)(2,1)} %pad_maximum_fusion.1.src_ref, s32[32,32768]{1,0:T(8,128)} %leaf_ref.1, f32[32,32768]{1,0:T(8,128)} %get-tuple-element.16.grad_ref, f32[32,32768]{1,0:T(8,128)} %get-tuple-element.20.hess_ref, ...), custom_call_target="tpu_custom_call" | custom-call | tf_op jit(solution)/shard_map/pallas_call | solution.py:398
  163.9 4.6 %copy.78 = f32[32,32768]{1,0:T(8,128)} copy(f32[32,32768]{1,0:T(8,128)} %get-tuple-element.36) | data formatting | bytes 8388608
  169.2 2.0 %copy.80 = bf16[2,128,1,8192]{3,1,2,0:T(8,128)(2,1)} copy(bf16[2,128,1,8192]{3,1,2,0:T(8,128)(2,1)S(1)} %bitcast.93) | data formatting | bytes 8388608
  (41 shorter events, 5.6 us)
Async XLA Ops:
  6.1 2.7 %copy-start.4 = (s32[32768]{0:T(1024)S(1)}, s32[32768]{0:T(1024)}, u32[]{:S(2)}) copy-start(s32[32768]{0:T(1024)} %param.7) | copy-start | bytes 393220
  16.5 2.0 %copy-start.2 = (f32[256,4,8,128]{3,2,1,0:T(8,128)}, f32[256,4,8,128]{3,2,1,0:T(8,128)S(1)}, u32[]{:S(2)}) copy-start(f32[256,4,8,128]{3,2,1,0:T(8,128)S(1)} %fusion.10) | copy-start | bytes 12582916
  74.9 2.0 %copy-start = (f32[256,4,8,128]{3,2,1,0:T(8,128)}, f32[256,4,8,128]{3,2,1,0:T(8,128)S(1)}, u32[]{:S(2)}) copy-start(f32[256,4,8,128]{3,2,1,0:T(8,128)S(1)} %get-tuple-element.23) | copy-start | bytes 12582916
  75.0 3.4 %copy-start.1 = (f32[256,4,8,128]{3,2,1,0:T(8,128)}, f32[256,4,8,128]{3,2,1,0:T(8,128)S(1)}, u32[]{:S(2)}) copy-start(f32[256,4,8,128]{3,2,1,0:T(8,128)S(1)} %get-tuple-element.24) | copy-start | bytes 12582916
  163.9 4.6 %copy-start.5 = (f32[32,64]{1,0:T(8,128)S(1)}, f32[32,64]{1,0:T(8,128)}, u32[]{:S(2)}) copy-start(f32[32,64]{1,0:T(8,128)} %get-tuple-element.37) | copy-start | bytes 24580
  163.9 5.2 %copy-start.3 = (bf16[2,128,8192]{2,1,0:T(8,128)(2,1)S(1)}, bf16[2,128,8192]{2,1,0:T(8,128)(2,1)}, u32[]{:S(2)}) copy-start(bf16[2,128,8192]{2,1,0:T(8,128)(2,1)} %get-tuple-element.8) | copy-start | bytes 12582916

commit v3 on v2

--- a/solution.py
+++ b/solution.py
@@ -420,6 +420,213 @@
     return grad_hess, leaf_weights, new_pred
 
 
+def tm_exchange(payload, held, send_sem, recv_sem, stage_sem, ep, me, n):
+    staged = pltpu.make_async_copy(payload, held.at[me], stage_sem)
+    staged.start()
+    staged.wait()
+
+    def copy_to(p):
+        return pltpu.make_async_remote_copy(
+            src_ref=held.at[me],
+            dst_ref=held.at[me],
+            send_sem=send_sem.at[p],
+            recv_sem=recv_sem.at[me],
+            device_id=(ep, p),
+            device_id_type=MESH,
+        )
+
+    def copy_from(p):
+        return pltpu.make_async_remote_copy(
+            src_ref=held.at[me],
+            dst_ref=held.at[p],
+            send_sem=send_sem.at[p],
+            recv_sem=recv_sem.at[p],
+            device_id=(ep, p),
+            device_id_type=MESH,
+        )
+
+    def send(k, carry):
+        copy_to(lax.rem(me + k, n)).start()
+        return carry
+
+    lax.fori_loop(1, n, send, 0)
+
+    def wait(k, carry):
+        p = lax.rem(me + k, n)
+        copy_to(p).wait_send()
+        copy_from(p).wait_recv()
+        return carry
+
+    lax.fori_loop(1, n, wait, 0)
+
+
+def scan_lanes(x, from_end):
+    lane = lax.broadcasted_iota(jnp.int32, x.shape, 1)
+    k = 1
+    while k < 128:
+        if from_end:
+            moved = pltpu.roll(x, 128 - k, 1)
+            x = x + jnp.where(lane < 128 - k, moved, 0.0)
+        else:
+            moved = pltpu.roll(x, k, 1)
+            x = x + jnp.where(lane >= k, moved, 0.0)
+        k *= 2
+    return x
+
+
+def front(predictions, events, first_rows, last_rows):
+    n = lax.axis_size("tm")
+    groups, length = predictions.shape
+    tiles = groups // 8
+    blocks = length // 128
+
+    def kernel(pred_ref, ev_ref, first_ref, last_ref,
+               grad_ref, hess_ref, both_ref,
+               weight, one, two, pay_a, held_a, pay_b, held_b,
+               send_a, recv_a, send_b, recv_b, stage):
+        me = lax.axis_index("tm")
+        ep = lax.axis_index("ep")
+        barrier = pltpu.get_barrier_semaphore()
+
+        def greet(k, carry):
+            p = lax.rem(me + k, n)
+            pl.semaphore_signal(barrier, inc=1, device_id=(ep, p), device_id_type=MESH)
+            return carry
+
+        lax.fori_loop(1, n, greet, 0)
+        pl.semaphore_wait(barrier, n - 1)
+
+        def suffix_tile(t, carry):
+            rows = pl.ds(pl.multiple_of(t * 8, 8), 8)
+
+            def one_block(j, later):
+                b = blocks - 1 - j
+                cols = pl.ds(pl.multiple_of(b * 128, 128), 128)
+                w = jnp.exp(pred_ref[rows, cols])
+                weight[rows, cols] = w
+                s = scan_lanes(w, True)
+                idx = first_ref[pl.ds(pl.multiple_of(b * 8, 8), 8), :]
+                one[rows, cols] = jnp.take_along_axis(s, idx, axis=1, mode="promise_in_bounds") + later
+                return later + jnp.broadcast_to(s[:, 0:1], (8, 128))
+
+            total = lax.fori_loop(0, blocks, one_block, jnp.zeros((8, 128), jnp.float32), unroll=4)
+            pay_a[rows, :] = total
+            return carry
+
+        lax.fori_loop(0, tiles, suffix_tile, 0)
+        tm_exchange(pay_a, held_a, send_a, recv_a, stage.at[0], ep, me, n)
+
+        def add_later(k, total):
+            p = lax.rem(me + k, n)
+            return total + jnp.where(p > me, held_a[p], 0.0)
+
+        pay_a[...] = lax.fori_loop(1, n, add_later, jnp.zeros((groups, 128), jnp.float32))
+
+        def prefix_tile(t, carry):
+            rows = pl.ds(pl.multiple_of(t * 8, 8), 8)
+            later = pay_a[rows, :]
+
+            def one_block(b, carries):
+                c1, c2 = carries
+                cols = pl.ds(pl.multiple_of(b * 128, 128), 128)
+                risk = one[rows, cols] + later
+                observed = ev_ref[rows, cols].astype(jnp.float32)
+                inv_one = observed / risk
+                inv_two = inv_one / risk
+                s1 = scan_lanes(inv_one, False)
+                s2 = scan_lanes(inv_two, False)
+                idx = last_ref[pl.ds(pl.multiple_of(b * 8, 8), 8), :]
+                one[rows, cols] = jnp.take_along_axis(s1, idx, axis=1, mode="promise_in_bounds") + c1
+                two[rows, cols] = jnp.take_along_axis(s2, idx, axis=1, mode="promise_in_bounds") + c2
+                return (
+                    c1 + jnp.broadcast_to(s1[:, 127:128], (8, 128)),
+                    c2 + jnp.broadcast_to(s2[:, 127:128], (8, 128)),
+                )
+
+            zero = jnp.zeros((8, 128), jnp.float32)
+            c1, c2 = lax.fori_loop(0, blocks, one_block, (zero, zero), unroll=4)
+            pay_b[rows, :] = c1
+            pay_b[pl.ds(pl.multiple_of(groups + t * 8, 8), 8), :] = c2
+            return carry
+
+        lax.fori_loop(0, tiles, prefix_tile, 0)
+        tm_exchange(pay_b, held_b, send_b, recv_b, stage.at[1], ep, me, n)
+
+        def add_earlier(k, total):
+            p = lax.rem(me + k, n)
+            return total + jnp.where(p < me, held_b[p], 0.0)
+
+        pay_b[...] = lax.fori_loop(1, n, add_earlier, jnp.zeros((2 * groups, 128), jnp.float32))
+
+        def out_tile(t, carry):
+            rows = pl.ds(pl.multiple_of(t * 8, 8), 8)
+            e1 = pay_b[rows, :]
+            e2 = pay_b[pl.ds(pl.multiple_of(groups + t * 8, 8), 8), :]
+
+            def one_block(b, carry):
+                cols = pl.ds(pl.multiple_of(b * 128, 128), 128)
+                w = weight[rows, cols]
+                a1 = one[rows, cols] + e1
+                a2 = two[rows, cols] + e2
+                observed = ev_ref[rows, cols].astype(jnp.float32)
+                g = w * a1 - observed
+                h = w * a1 - w * w * a2
+                grad_ref[rows, cols] = g
+                hess_ref[rows, cols] = h
+                both_ref[0, rows, cols] = g.astype(jnp.bfloat16)
+                both_ref[1, rows, cols] = h.astype(jnp.bfloat16)
+                return carry
+
+            lax.fori_loop(0, blocks, one_block, 0, unroll=4)
+            return carry
+
+        lax.fori_loop(0, tiles, out_tile, 0)
+
+    vmem = pl.BlockSpec(memory_space=pltpu.VMEM)
+    return pl.pallas_call(
+        kernel,
+        out_shape=(
+            jax.ShapeDtypeStruct((groups, length), jnp.float32),
+            jax.ShapeDtypeStruct((groups, length), jnp.float32),
+            jax.ShapeDtypeStruct((2, groups, length), jnp.bfloat16),
+        ),
+        in_specs=[vmem, vmem, vmem, vmem],
+        out_specs=(vmem, vmem, vmem),
+        scratch_shapes=[
+            pltpu.VMEM((groups, length), jnp.float32),
+            pltpu.VMEM((groups, length), jnp.float32),
+            pltpu.VMEM((groups, length), jnp.float32),
+            pltpu.VMEM((groups, 128), jnp.float32),
+            pltpu.VMEM((n, groups, 128), jnp.float32),
+            pltpu.VMEM((2 * groups, 128), jnp.float32),
+            pltpu.VMEM((n, 2 * groups, 128), jnp.float32),
+            pltpu.SemaphoreType.DMA((n,)),
+            pltpu.SemaphoreType.DMA((n,)),
+            pltpu.SemaphoreType.DMA((n,)),
+            pltpu.SemaphoreType.DMA((n,)),
+            pltpu.SemaphoreType.DMA((2,)),
+        ],
+        compiler_params=pltpu.CompilerParams(
+            collective_id=0, has_side_effects=True, vmem_limit_bytes=60 * 1024 * 1024
+        ),
+    )(predictions, events, first_rows, last_rows)
+
+
+def tie_rows(tie_start):
+    length = tie_start.shape[0]
+    blocks = length // 128
+    starts = tie_start.reshape(blocks, 128)
+    labels = jnp.arange(128, dtype=jnp.int32)
+    first_local = lax.cummax(jnp.where(starts == 1, labels[None, :], 0), axis=1)
+    next_start = jnp.concatenate([starts[:, 1:], jnp.ones((blocks, 1), jnp.int32)], axis=1)
+    last_local = lax.cummin(jnp.where(next_start == 1, labels[None, :], 127), axis=1, reverse=True)
+
+    def spread(rows):
+        return jnp.broadcast_to(rows[:, None, :], (blocks, 8, 128)).reshape(blocks * 8, 128)
+
+    return spread(first_local), spread(last_local)
+
+
 def lane_pad(vectors):
     width = vectors.shape[1]
     return jnp.pad(vectors, ((0, 0), (0, 128 - width)))
@@ -479,27 +686,8 @@
 
 
 def on_device(predictions, leaf_index, events, tie_start):
-    groups = predictions.shape[0]
-    length = predictions.shape[1]
-    backward, forward = tile_matrices(tie_start)
-    weight = jnp.exp(predictions)
-    local_risk = block_cumsum(weight, backward, True)
-    block_total = local_risk[:, 0]
-    later_total = tm_combine(lane_pad(block_total[None, :]), "later", 0)[0, :groups]
-    risk = local_risk + later_total[:, None]
-    observed = events.astype(jnp.float32)
-    inv_one = observed / risk
-    inv_two = inv_one / risk
-    local_both = block_cumsum(jnp.concatenate([inv_one, inv_two]), forward, False)
-    local_one = local_both[:groups]
-    local_two = local_both[groups:]
-    pair = lane_pad(jnp.stack([local_one[:, -1], local_two[:, -1]]))
-    earlier = tm_combine(pair, "earlier", 1)
-    accum_one = local_one + earlier[0, :groups][:, None]
-    accum_two = local_two + earlier[1, :groups][:, None]
-    gradient = weight * accum_one - observed
-    hessian = weight * accum_one - weight * weight * accum_two
-    stacked = jnp.stack([gradient, hessian]).astype(jnp.bfloat16)
+    first_rows, last_rows = tie_rows(tie_start)
+    gradient, hessian, stacked = front(predictions, events, first_rows, last_rows)
     grad_hess, leaf_weights, new_pred = finish(
         stacked, leaf_index, gradient, hessian, predictions, LEAVES, 2
     )

time: 171 us -> 852 us (4.98)
  Pallas kernels: 84.8 us -> 836 us
  other arithmetic: 41.8 us -> 5.5 us
  local copies, waits for them, and re-layouts: 28.1 us -> 10.1 us
  matrix products: 15.5 us -> 0 us
    pallas_call x2 -> x1, Pallas kernels: 23.7 us -> 771 us  [front(): pl.pallas_call(kernel, out_shape=(jax.ShapeDtypeStruct((groups, length),...]
    unnamed x19 -> x7, local copies, waits for them, and re-layouts: 23.4 us -> 7.25 us
    dot_general x2 -> x0, matrix products: 15.5 us -> none  [block_cumsum(): jnp.einsum('ebj,bji->ebi', shaped, matrices, precision=lax.Precision.HIGH)]
    another operation x10 -> x2, other arithmetic: 19.2 us -> 4.56 us  [the longest x1 4.39 us: tie_rows(): lax.cummin(jnp.where(next_start == 1, labels[None, :], 127), axis=1, reve...]
    unnamed x1 -> x0, other arithmetic: 11.2 us -> none
where the time goes in v3:
time: 852 us
  Pallas kernels  836 us (98%)
  local copies, waits for them, and re-layouts  10.1 us (1%)
    pallas_call x1, Pallas kernels, front(): pl.pallas_call(kernel, out_shape=(jax.ShapeDtypeStruct((groups, length),...  771 us
    pallas_call x1, Pallas kernels, finish(): pl.pallas_call(kernel, out_shape=(jax.ShapeDtypeStruct((two, groups * m,...  64.6 us

profile of v3, /device:TPU:1, one launch (start us, length us, event | category | flops | bytes accessed | tf_op | source)
XLA Modules:
  0.0 852.1 jit_solution(4683593390420711882)
XLA Ops:
  0.6 1.0 slice.4
  1.7 0.1 copy.12
  1.8 4.4 reduce_window_min.10
  6.1 0.1 copy.13
  6.2 0.9 iota_select_fusion.1
  7.2 0.1 copy.10
  7.3 0.2 reduce_window_max.10
  7.4 0.1 copy.11
  7.5 1.5 broadcast_bitcast_fusion
  9.0 771.2 %shard_map.67 = (f32[32,32768]{1,0:T(8,128)}, f32[32,32768]{1,0:T(8,128)}, bf16[2,32,32768]{2,1,0:T(8,128)(2,1)}) custom-call(f32[32,32768]{1,0:T(8,128)} %pred_ref.3, s32[32,32768]{1,0:T(8,128)} %ev_ref.1, s32[2048,128]{1,0:T(8,128)} %get-tuple-element.22.first_ref, s32[2048,128]{1,0:T(8,128)} %get-tuple-element.21.last_ref), custom_call_target="tpu_custom_call" | custom-call | tf_op jit(solution)/shard_map/pallas_call | solution.py:586
  780.2 64.6 %shard_map.68 = (bf16[2,128,8192]{2,1,0:T(8,128)(2,1)}, f32[32,64]{1,0:T(8,128)}, f32[32,32768]{1,0:T(8,128)}) custom-call(bf16[2,32,32768]{2,1,0:T(8,128)(2,1)} %get-tuple-element.9.src_ref, s32[32,32768]{1,0:T(8,128)} %leaf_ref.1, f32[32,32768]{1,0:T(8,128)} %get-tuple-element.10.grad_ref, f32[32,32768]{1,0:T(8,128)} %get-tuple-element.11.hess_ref, ...), custom_call_target="tpu_custom_call" | custom-call | tf_op jit(solution)/shard_map/pallas_call | solution.py:398
  844.8 0.0 copy-start.1
  844.8 0.0 copy-start
  844.8 4.6 copy.18
  849.5 0.0 copy-done.1
  849.5 0.6 copy.19
  850.1 0.0 copy-done
  850.1 2.0 copy.20
  (1 shorter events, 0.0 us)
Async XLA Ops:
  844.8 4.6 copy-start.1
  844.8 5.2 copy-start

commit v4 on v3

--- a/solution.py
+++ b/solution.py
@@ -479,6 +479,8 @@
     groups, length = predictions.shape
     tiles = groups // 8
     blocks = length // 128
+    span = math.gcd(blocks, 8)
+    groups_n = blocks // span
 
     def kernel(pred_ref, ev_ref, first_ref, last_ref,
                grad_ref, hess_ref, both_ref,
@@ -496,20 +498,42 @@
         lax.fori_loop(1, n, greet, 0)
         pl.semaphore_wait(barrier, n - 1)
 
+        lane_j = lax.broadcasted_iota(jnp.int32, (128, 128), 0)
+        lane_i = lax.broadcasted_iota(jnp.int32, (128, 128), 1)
+        upper = (lane_j >= lane_i).astype(jnp.bfloat16)
+        lower = (lane_j <= lane_i).astype(jnp.bfloat16)
+
+        def run_sum(x, matrix):
+            hi = x.astype(jnp.bfloat16)
+            rest = x - hi.astype(jnp.float32)
+            mid = rest.astype(jnp.bfloat16)
+            lo = (rest - mid.astype(jnp.float32)).astype(jnp.bfloat16)
+            out = jnp.dot(hi, matrix, preferred_element_type=jnp.float32)
+            out = out + jnp.dot(mid, matrix, preferred_element_type=jnp.float32)
+            return out + jnp.dot(lo, matrix, preferred_element_type=jnp.float32)
+
+        def block_cols(b):
+            return pl.ds(pl.multiple_of(b * 128, 128), 128)
+
         def suffix_tile(t, carry):
             rows = pl.ds(pl.multiple_of(t * 8, 8), 8)
 
-            def one_block(j, later):
-                b = blocks - 1 - j
-                cols = pl.ds(pl.multiple_of(b * 128, 128), 128)
-                w = jnp.exp(pred_ref[rows, cols])
-                weight[rows, cols] = w
-                s = scan_lanes(w, True)
-                idx = first_ref[pl.ds(pl.multiple_of(b * 8, 8), 8), :]
-                one[rows, cols] = jnp.take_along_axis(s, idx, axis=1, mode="promise_in_bounds") + later
-                return later + jnp.broadcast_to(s[:, 0:1], (8, 128))
-
-            total = lax.fori_loop(0, blocks, one_block, jnp.zeros((8, 128), jnp.float32), unroll=4)
+            def one_group(j, later):
+                b0 = (groups_n - 1 - j) * span
+                pieces = []
+                for k in range(span):
+                    w = jnp.exp(pred_ref[rows, block_cols(b0 + k)])
+                    weight[rows, block_cols(b0 + k)] = w
+                    pieces.append(w)
+                s = run_sum(jnp.concatenate(pieces, axis=0), upper)
+                idx = first_ref[pl.ds(pl.multiple_of(b0 * 8, 8), 8 * span), :]
+                r = jnp.take_along_axis(s, idx, axis=1, mode="promise_in_bounds")
+                for k in reversed(range(span)):
+                    one[rows, block_cols(b0 + k)] = r[8 * k:8 * k + 8] + later
+                    later = later + jnp.broadcast_to(s[8 * k:8 * k + 8, 0:1], (8, 128))
+                return later
+
+            total = lax.fori_loop(0, groups_n, one_group, jnp.zeros((8, 128), jnp.float32))
             pay_a[rows, :] = total
             return carry
 
@@ -526,25 +550,30 @@
             rows = pl.ds(pl.multiple_of(t * 8, 8), 8)
             later = pay_a[rows, :]
 
-            def one_block(b, carries):
+            def one_group(j, carries):
                 c1, c2 = carries
-                cols = pl.ds(pl.multiple_of(b * 128, 128), 128)
-                risk = one[rows, cols] + later
-                observed = ev_ref[rows, cols].astype(jnp.float32)
-                inv_one = observed / risk
-                inv_two = inv_one / risk
-                s1 = scan_lanes(inv_one, False)
-                s2 = scan_lanes(inv_two, False)
-                idx = last_ref[pl.ds(pl.multiple_of(b * 8, 8), 8), :]
-                one[rows, cols] = jnp.take_along_axis(s1, idx, axis=1, mode="promise_in_bounds") + c1
-                two[rows, cols] = jnp.take_along_axis(s2, idx, axis=1, mode="promise_in_bounds") + c2
-                return (
-                    c1 + jnp.broadcast_to(s1[:, 127:128], (8, 128)),
-                    c2 + jnp.broadcast_to(s2[:, 127:128], (8, 128)),
-                )
+                b0 = j * span
+                firsts, seconds = [], []
+                for k in range(span):
+                    risk = one[rows, block_cols(b0 + k)] + later
+                    observed = ev_ref[rows, block_cols(b0 + k)].astype(jnp.float32)
+                    inv_one = observed / risk
+                    firsts.append(inv_one)
+                    seconds.append(inv_one / risk)
+                s = run_sum(jnp.concatenate(firsts + seconds, axis=0), lower)
+                idx = last_ref[pl.ds(pl.multiple_of(b0 * 8, 8), 8 * span), :]
+                idx = jnp.concatenate([idx, idx], axis=0)
+                r = jnp.take_along_axis(s, idx, axis=1, mode="promise_in_bounds")
+                half = 8 * span
+                for k in range(span):
+                    one[rows, block_cols(b0 + k)] = r[8 * k:8 * k + 8] + c1
+                    two[rows, block_cols(b0 + k)] = r[half + 8 * k:half + 8 * k + 8] + c2
+                    c1 = c1 + jnp.broadcast_to(s[8 * k:8 * k + 8, 127:128], (8, 128))
+                    c2 = c2 + jnp.broadcast_to(s[half + 8 * k:half + 8 * k + 8, 127:128], (8, 128))
+                return (c1, c2)
 
             zero = jnp.zeros((8, 128), jnp.float32)
-            c1, c2 = lax.fori_loop(0, blocks, one_block, (zero, zero), unroll=4)
+            c1, c2 = lax.fori_loop(0, groups_n, one_group, (zero, zero))
             pay_b[rows, :] = c1
             pay_b[pl.ds(pl.multiple_of(groups + t * 8, 8), 8), :] = c2
             return carry
@@ -560,11 +589,11 @@
 
         def out_tile(t, carry):
             rows = pl.ds(pl.multiple_of(t * 8, 8), 8)
-            e1 = pay_b[rows, :]
-            e2 = pay_b[pl.ds(pl.multiple_of(groups + t * 8, 8), 8), :]
-
-            def one_block(b, carry):
-                cols = pl.ds(pl.multiple_of(b * 128, 128), 128)
+            e1 = jnp.tile(pay_b[rows, :], (1, span))
+            e2 = jnp.tile(pay_b[pl.ds(pl.multiple_of(groups + t * 8, 8), 8), :], (1, span))
+
+            def one_group(j, carry):
+                cols = pl.ds(pl.multiple_of(j * span * 128, span * 128), span * 128)
                 w = weight[rows, cols]
                 a1 = one[rows, cols] + e1
                 a2 = two[rows, cols] + e2
@@ -577,7 +606,7 @@
                 both_ref[1, rows, cols] = h.astype(jnp.bfloat16)
                 return carry
 
-            lax.fori_loop(0, blocks, one_block, 0, unroll=4)
+            lax.fori_loop(0, groups_n, one_group, 0)
             return carry
 
         lax.fori_loop(0, tiles, out_tile, 0)

time: 852 us -> 195 us (0.23)
  Pallas kernels: 836 us -> 179 us
    pallas_call x1, Pallas kernels: 771 us -> 114 us  [front(): pl.pallas_call(kernel, out_shape=(jax.ShapeDtypeStruct((groups, length),...]
where the time goes in v4:
time: 195 us
  Pallas kernels  179 us (92%)
  local copies, waits for them, and re-layouts  10.1 us (5%)
  other arithmetic  5.5 us (3%)
    pallas_call x1, Pallas kernels, front(): pl.pallas_call(kernel, out_shape=(jax.ShapeDtypeStruct((groups, length),...  114 us
    pallas_call x1, Pallas kernels, finish(): pl.pallas_call(kernel, out_shape=(jax.ShapeDtypeStruct((two, groups * m,...  64.6 us
    unnamed x7, local copies, waits for them, and re-layouts  7.25 us
    another operation x1, other arithmetic, tie_rows(): lax.cummin(jnp.where(next_start == 1, labels[None, :], 127), axis=1, reve...  4.39 us

profile of v4, /device:TPU:1, one launch (start us, length us, event | category | flops | bytes accessed | tf_op | source)
XLA Modules:
  0.0 195.2 jit_solution(16929616779497522546)
XLA Ops:
  0.6 1.0 slice.4
  1.7 0.1 copy.12
  1.8 4.4 %reduce_window_min.10 = s32[256,128]{0,1:T(8,128)S(1)} reduce-window(s32[256,128]{0,1:T(8,128)S(1)} %copy.12, s32[]{:T(128)} %constant.12.clone.1), window={size=1x128 pad=0_0x0_127}, to_apply=%region_1.2 | reduce-window | flops 4161536 | bytes 262148 | tf_op jit(solution)/shard_map/tie_rows/reduce_window_min | solution.py:651
  6.1 0.1 copy.13
  6.2 0.9 iota_select_fusion.1
  7.2 0.1 copy.10
  7.3 0.2 reduce_window_max.10
  7.4 0.1 copy.11
  7.5 1.5 broadcast_bitcast_fusion
  9.0 114.3 %shard_map.67 = (f32[32,32768]{1,0:T(8,128)}, f32[32,32768]{1,0:T(8,128)}, bf16[2,32,32768]{2,1,0:T(8,128)(2,1)}) custom-call(f32[32,32768]{1,0:T(8,128)} %pred_ref.3, s32[32,32768]{1,0:T(8,128)} %ev_ref.1, s32[2048,128]{1,0:T(8,128)} %get-tuple-element.22.first_ref, s32[2048,128]{1,0:T(8,128)} %get-tuple-element.21.last_ref), custom_call_target="tpu_custom_call" | custom-call | tf_op jit(solution)/shard_map/pallas_call | solution.py:615
  123.3 64.6 %shard_map.68 = (bf16[2,128,8192]{2,1,0:T(8,128)(2,1)}, f32[32,64]{1,0:T(8,128)}, f32[32,32768]{1,0:T(8,128)}) custom-call(bf16[2,32,32768]{2,1,0:T(8,128)(2,1)} %get-tuple-element.9.src_ref, s32[32,32768]{1,0:T(8,128)} %leaf_ref.1, f32[32,32768]{1,0:T(8,128)} %get-tuple-element.10.grad_ref, f32[32,32768]{1,0:T(8,128)} %get-tuple-element.11.hess_ref, ...), custom_call_target="tpu_custom_call" | custom-call | tf_op jit(solution)/shard_map/pallas_call | solution.py:398
  187.9 0.0 copy-start.1
  187.9 0.0 copy-start
  187.9 4.6 %copy.18 = f32[32,32768]{1,0:T(8,128)} copy(f32[32,32768]{1,0:T(8,128)} %get-tuple-element.26) | data formatting | bytes 8388608
  192.6 0.0 copy-done.1
  192.6 0.6 copy.19
  193.2 0.0 copy-done
  193.2 2.0 %copy.20 = bf16[2,128,1,8192]{3,1,2,0:T(8,128)(2,1)} copy(bf16[2,128,1,8192]{3,1,2,0:T(8,128)(2,1)S(1)} %bitcast.9) | data formatting | bytes 8388608
  (1 shorter events, 0.0 us)
Async XLA Ops:
  187.9 4.6 %copy-start.1 = (f32[32,64]{1,0:T(8,128)S(1)}, f32[32,64]{1,0:T(8,128)}, u32[]{:S(2)}) copy-start(f32[32,64]{1,0:T(8,128)} %get-tuple-element.27) | copy-start | bytes 24580
  187.9 5.2 %copy-start = (bf16[2,128,8192]{2,1,0:T(8,128)(2,1)S(1)}, bf16[2,128,8192]{2,1,0:T(8,128)(2,1)}, u32[]{:S(2)}) copy-start(bf16[2,128,8192]{2,1,0:T(8,128)(2,1)} %get-tuple-element.14) | copy-start | bytes 12582916

commit v5 on v4

--- a/solution.py
+++ b/solution.py
@@ -479,7 +479,7 @@
     groups, length = predictions.shape
     tiles = groups // 8
     blocks = length // 128
-    span = math.gcd(blocks, 8)
+    span = math.gcd(blocks, 16)
     groups_n = blocks // span
 
     def kernel(pred_ref, ev_ref, first_ref, last_ref,
@@ -533,7 +533,7 @@
                     later = later + jnp.broadcast_to(s[8 * k:8 * k + 8, 0:1], (8, 128))
                 return later
 
-            total = lax.fori_loop(0, groups_n, one_group, jnp.zeros((8, 128), jnp.float32))
+            total = lax.fori_loop(0, groups_n, one_group, jnp.zeros((8, 128), jnp.float32), unroll=2)
             pay_a[rows, :] = total
             return carry
 
@@ -573,7 +573,7 @@
                 return (c1, c2)
 
             zero = jnp.zeros((8, 128), jnp.float32)
-            c1, c2 = lax.fori_loop(0, groups_n, one_group, (zero, zero))
+            c1, c2 = lax.fori_loop(0, groups_n, one_group, (zero, zero), unroll=2)
             pay_b[rows, :] = c1
             pay_b[pl.ds(pl.multiple_of(groups + t * 8, 8), 8), :] = c2
             return carry

time: 195 us -> 163 us (0.84)
  Pallas kernels: 179 us -> 147 us
    pallas_call x1, Pallas kernels: 114 us -> 81.6 us  [front(): pl.pallas_call(kernel, out_shape=(jax.ShapeDtypeStruct((groups, length),...]
where the time goes in v5:
time: 163 us
  Pallas kernels  147 us (90%)
  local copies, waits for them, and re-layouts  10.1 us (6%)
  other arithmetic  5.5 us (3%)
    pallas_call x1, Pallas kernels, front(): pl.pallas_call(kernel, out_shape=(jax.ShapeDtypeStruct((groups, length),...  81.6 us
    pallas_call x1, Pallas kernels, finish(): pl.pallas_call(kernel, out_shape=(jax.ShapeDtypeStruct((two, groups * m,...  65.1 us
    unnamed x7, local copies, waits for them, and re-layouts  7.25 us
    another operation x1, other arithmetic, tie_rows(): lax.cummin(jnp.where(next_start == 1, labels[None, :], 127), axis=1, reve...  4.39 us

profile of v5, /device:TPU:1, one launch (start us, length us, event | category | flops | bytes accessed | tf_op | source)
XLA Modules:
  0.0 163.0 jit_solution(8387339096694996927)
XLA Ops:
  0.6 1.0 slice.4
  1.7 0.1 copy.12
  1.8 4.4 %reduce_window_min.10 = s32[256,128]{0,1:T(8,128)S(1)} reduce-window(s32[256,128]{0,1:T(8,128)S(1)} %copy.12, s32[]{:T(128)} %constant.12.clone.1), window={size=1x128 pad=0_0x0_127}, to_apply=%region_1.2 | reduce-window | flops 4161536 | bytes 262148 | tf_op jit(solution)/shard_map/tie_rows/reduce_window_min | solution.py:651
  6.1 0.1 copy.13
  6.2 0.9 iota_select_fusion.1
  7.2 0.1 copy.10
  7.3 0.2 reduce_window_max.10
  7.4 0.1 copy.11
  7.5 1.5 broadcast_bitcast_fusion
  9.0 81.6 %shard_map.67 = (f32[32,32768]{1,0:T(8,128)}, f32[32,32768]{1,0:T(8,128)}, bf16[2,32,32768]{2,1,0:T(8,128)(2,1)}) custom-call(f32[32,32768]{1,0:T(8,128)} %pred_ref.3, s32[32,32768]{1,0:T(8,128)} %ev_ref.1, s32[2048,128]{1,0:T(8,128)} %get-tuple-element.22.first_ref, s32[2048,128]{1,0:T(8,128)} %get-tuple-element.21.last_ref), custom_call_target="tpu_custom_call" | custom-call | tf_op jit(solution)/shard_map/pallas_call | solution.py:615
  90.6 65.1 %shard_map.68 = (bf16[2,128,8192]{2,1,0:T(8,128)(2,1)}, f32[32,64]{1,0:T(8,128)}, f32[32,32768]{1,0:T(8,128)}) custom-call(bf16[2,32,32768]{2,1,0:T(8,128)(2,1)} %get-tuple-element.9.src_ref, s32[32,32768]{1,0:T(8,128)} %leaf_ref.1, f32[32,32768]{1,0:T(8,128)} %get-tuple-element.10.grad_ref, f32[32,32768]{1,0:T(8,128)} %get-tuple-element.11.hess_ref, ...), custom_call_target="tpu_custom_call" | custom-call | tf_op jit(solution)/shard_map/pallas_call | solution.py:398
  155.7 0.0 copy-start.1
  155.8 0.0 copy-start
  155.8 4.6 %copy.18 = f32[32,32768]{1,0:T(8,128)} copy(f32[32,32768]{1,0:T(8,128)} %get-tuple-element.26) | data formatting | bytes 8388608
  160.4 0.0 copy-done.1
  160.4 0.6 copy.19
  161.0 0.0 copy-done
  161.0 2.0 %copy.20 = bf16[2,128,1,8192]{3,1,2,0:T(8,128)(2,1)} copy(bf16[2,128,1,8192]{3,1,2,0:T(8,128)(2,1)S(1)} %bitcast.9) | data formatting | bytes 8388608
  (1 shorter events, 0.0 us)
Async XLA Ops:
  155.7 4.6 %copy-start.1 = (f32[32,64]{1,0:T(8,128)S(1)}, f32[32,64]{1,0:T(8,128)}, u32[]{:S(2)}) copy-start(f32[32,64]{1,0:T(8,128)} %get-tuple-element.27) | copy-start | bytes 24580
  155.8 5.2 %copy-start = (bf16[2,128,8192]{2,1,0:T(8,128)(2,1)S(1)}, bf16[2,128,8192]{2,1,0:T(8,128)(2,1)}, u32[]{:S(2)}) copy-start(bf16[2,128,8192]{2,1,0:T(8,128)(2,1)} %get-tuple-element.14) | copy-start | bytes 12582916

commit v6 on v5

--- a/solution.py
+++ b/solution.py
@@ -479,7 +479,7 @@
     groups, length = predictions.shape
     tiles = groups // 8
     blocks = length // 128
-    span = math.gcd(blocks, 16)
+    span = math.gcd(blocks, 32)
     groups_n = blocks // span
 
     def kernel(pred_ref, ev_ref, first_ref, last_ref,

time: 163 us -> 154 us (0.945)
  Pallas kernels: 147 us -> 137 us
    pallas_call x1, Pallas kernels: 81.6 us -> 72.3 us  [front(): pl.pallas_call(kernel, out_shape=(jax.ShapeDtypeStruct((groups, length),...]
where the time goes in v6:
time: 154 us
  Pallas kernels  137 us (89%)
  local copies, waits for them, and re-layouts  10.1 us (7%)
  other arithmetic  5.5 us (4%)
    pallas_call x1, Pallas kernels, front(): pl.pallas_call(kernel, out_shape=(jax.ShapeDtypeStruct((groups, length),...  72.3 us
    pallas_call x1, Pallas kernels, finish(): pl.pallas_call(kernel, out_shape=(jax.ShapeDtypeStruct((two, groups * m,...  65.1 us
    unnamed x7, local copies, waits for them, and re-layouts  7.25 us
    another operation x1, other arithmetic, tie_rows(): lax.cummin(jnp.where(next_start == 1, labels[None, :], 127), axis=1, reve...  4.39 us

profile of v6, /device:TPU:1, one launch (start us, length us, event | category | flops | bytes accessed | tf_op | source)
XLA Modules:
  0.0 153.8 jit_solution(1639595447198413616)
XLA Ops:
  0.6 1.0 slice.4
  1.7 0.1 copy.12
  1.8 4.4 %reduce_window_min.10 = s32[256,128]{0,1:T(8,128)S(1)} reduce-window(s32[256,128]{0,1:T(8,128)S(1)} %copy.12, s32[]{:T(128)} %constant.12.clone.1), window={size=1x128 pad=0_0x0_127}, to_apply=%region_1.2 | reduce-window | flops 4161536 | bytes 262148 | tf_op jit(solution)/shard_map/tie_rows/reduce_window_min | solution.py:651
  6.1 0.1 copy.13
  6.2 0.9 iota_select_fusion.1
  7.2 0.1 copy.10
  7.3 0.2 reduce_window_max.10
  7.4 0.1 copy.11
  7.5 1.5 broadcast_bitcast_fusion
  9.0 72.3 %shard_map.67 = (f32[32,32768]{1,0:T(8,128)}, f32[32,32768]{1,0:T(8,128)}, bf16[2,32,32768]{2,1,0:T(8,128)(2,1)}) custom-call(f32[32,32768]{1,0:T(8,128)} %pred_ref.3, s32[32,32768]{1,0:T(8,128)} %ev_ref.1, s32[2048,128]{1,0:T(8,128)} %get-tuple-element.22.first_ref, s32[2048,128]{1,0:T(8,128)} %get-tuple-element.21.last_ref), custom_call_target="tpu_custom_call" | custom-call | tf_op jit(solution)/shard_map/pallas_call | solution.py:615
  81.3 65.1 %shard_map.68 = (bf16[2,128,8192]{2,1,0:T(8,128)(2,1)}, f32[32,64]{1,0:T(8,128)}, f32[32,32768]{1,0:T(8,128)}) custom-call(bf16[2,32,32768]{2,1,0:T(8,128)(2,1)} %get-tuple-element.9.src_ref, s32[32,32768]{1,0:T(8,128)} %leaf_ref.1, f32[32,32768]{1,0:T(8,128)} %get-tuple-element.10.grad_ref, f32[32,32768]{1,0:T(8,128)} %get-tuple-element.11.hess_ref, ...), custom_call_target="tpu_custom_call" | custom-call | tf_op jit(solution)/shard_map/pallas_call | solution.py:398
  146.5 0.0 copy-start.1
  146.5 0.0 copy-start
  146.5 4.6 %copy.18 = f32[32,32768]{1,0:T(8,128)} copy(f32[32,32768]{1,0:T(8,128)} %get-tuple-element.26) | data formatting | bytes 8388608
  151.1 0.0 copy-done.1
  151.1 0.6 copy.19
  151.8 0.0 copy-done
  151.8 2.0 %copy.20 = bf16[2,128,1,8192]{3,1,2,0:T(8,128)(2,1)} copy(bf16[2,128,1,8192]{3,1,2,0:T(8,128)(2,1)S(1)} %bitcast.9) | data formatting | bytes 8388608
  (1 shorter events, 0.0 us)
Async XLA Ops:
  146.5 4.6 %copy-start.1 = (f32[32,64]{1,0:T(8,128)S(1)}, f32[32,64]{1,0:T(8,128)}, u32[]{:S(2)}) copy-start(f32[32,64]{1,0:T(8,128)} %get-tuple-element.27) | copy-start | bytes 24580
  146.5 5.2 %copy-start = (bf16[2,128,8192]{2,1,0:T(8,128)(2,1)S(1)}, bf16[2,128,8192]{2,1,0:T(8,128)(2,1)}, u32[]{:S(2)}) copy-start(bf16[2,128,8192]{2,1,0:T(8,128)(2,1)} %get-tuple-element.14) | copy-start | bytes 12582916

commit v7 on v5

--- a/solution.py
+++ b/solution.py
@@ -515,29 +515,30 @@
         def block_cols(b):
             return pl.ds(pl.multiple_of(b * 128, 128), 128)
 
-        def suffix_tile(t, carry):
-            rows = pl.ds(pl.multiple_of(t * 8, 8), 8)
-
-            def one_group(j, later):
-                b0 = (groups_n - 1 - j) * span
+        def suffix_group(j, carries):
+            b0 = (groups_n - 1 - j) * span
+            idx = first_ref[pl.ds(pl.multiple_of(b0 * 8, 8), 8 * span), :]
+            out = []
+            for t in range(tiles):
+                rows = pl.ds(t * 8, 8)
+                later = carries[t]
                 pieces = []
                 for k in range(span):
                     w = jnp.exp(pred_ref[rows, block_cols(b0 + k)])
                     weight[rows, block_cols(b0 + k)] = w
                     pieces.append(w)
                 s = run_sum(jnp.concatenate(pieces, axis=0), upper)
-                idx = first_ref[pl.ds(pl.multiple_of(b0 * 8, 8), 8 * span), :]
                 r = jnp.take_along_axis(s, idx, axis=1, mode="promise_in_bounds")
                 for k in reversed(range(span)):
                     one[rows, block_cols(b0 + k)] = r[8 * k:8 * k + 8] + later
                     later = later + jnp.broadcast_to(s[8 * k:8 * k + 8, 0:1], (8, 128))
-                return later
-
-            total = lax.fori_loop(0, groups_n, one_group, jnp.zeros((8, 128), jnp.float32), unroll=2)
-            pay_a[rows, :] = total
-            return carry
-
-        lax.fori_loop(0, tiles, suffix_tile, 0)
+                out.append(later)
+            return tuple(out)
+
+        zero = jnp.zeros((8, 128), jnp.float32)
+        totals = lax.fori_loop(0, groups_n, suffix_group, (zero,) * tiles)
+        for t in range(tiles):
+            pay_a[pl.ds(t * 8, 8), :] = totals[t]
         tm_exchange(pay_a, held_a, send_a, recv_a, stage.at[0], ep, me, n)
 
         def add_later(k, total):
@@ -546,13 +547,16 @@
 
         pay_a[...] = lax.fori_loop(1, n, add_later, jnp.zeros((groups, 128), jnp.float32))
 
-        def prefix_tile(t, carry):
-            rows = pl.ds(pl.multiple_of(t * 8, 8), 8)
-            later = pay_a[rows, :]
-
-            def one_group(j, carries):
-                c1, c2 = carries
-                b0 = j * span
+        def prefix_group(j, carries):
+            b0 = j * span
+            idx = last_ref[pl.ds(pl.multiple_of(b0 * 8, 8), 8 * span), :]
+            idx = jnp.concatenate([idx, idx], axis=0)
+            half = 8 * span
+            out = []
+            for t in range(tiles):
+                rows = pl.ds(t * 8, 8)
+                later = pay_a[rows, :]
+                c1, c2 = carries[2 * t], carries[2 * t + 1]
                 firsts, seconds = [], []
                 for k in range(span):
                     risk = one[rows, block_cols(b0 + k)] + later
@@ -561,24 +565,19 @@
                     firsts.append(inv_one)
                     seconds.append(inv_one / risk)
                 s = run_sum(jnp.concatenate(firsts + seconds, axis=0), lower)
-                idx = last_ref[pl.ds(pl.multiple_of(b0 * 8, 8), 8 * span), :]
-                idx = jnp.concatenate([idx, idx], axis=0)
                 r = jnp.take_along_axis(s, idx, axis=1, mode="promise_in_bounds")
-                half = 8 * span
                 for k in range(span):
                     one[rows, block_cols(b0 + k)] = r[8 * k:8 * k + 8] + c1
                     two[rows, block_cols(b0 + k)] = r[half + 8 * k:half + 8 * k + 8] + c2
                     c1 = c1 + jnp.broadcast_to(s[8 * k:8 * k + 8, 127:128], (8, 128))
                     c2 = c2 + jnp.broadcast_to(s[half + 8 * k:half + 8 * k + 8, 127:128], (8, 128))
-                return (c1, c2)
-
-            zero = jnp.zeros((8, 128), jnp.float32)
-            c1, c2 = lax.fori_loop(0, groups_n, one_group, (zero, zero), unroll=2)
-            pay_b[rows, :] = c1
-            pay_b[pl.ds(pl.multiple_of(groups + t * 8, 8), 8), :] = c2
-            return carry
-
-        lax.fori_loop(0, tiles, prefix_tile, 0)
+                out += [c1, c2]
+            return tuple(out)
+
+        sums = lax.fori_loop(0, groups_n, prefix_group, (zero,) * (2 * tiles))
+        for t in range(tiles):
+            pay_b[pl.ds(t * 8, 8), :] = sums[2 * t]
+            pay_b[pl.ds(groups + t * 8, 8), :] = sums[2 * t + 1]
         tm_exchange(pay_b, held_b, send_b, recv_b, stage.at[1], ep, me, n)
 
         def add_earlier(k, total):

time: 163 us -> 157 us (0.963)
  Pallas kernels: 147 us -> 141 us
    pallas_call x1, Pallas kernels: 81.6 us -> 75.8 us  [front(): pl.pallas_call(kernel, out_shape=(jax.ShapeDtypeStruct((groups, length),...]
where the time goes in v7:
time: 157 us
  Pallas kernels  141 us (90%)
  local copies, waits for them, and re-layouts  10.1 us (6%)
  other arithmetic  5.5 us (4%)
    pallas_call x1, Pallas kernels, front(): pl.pallas_call(kernel, out_shape=(jax.ShapeDtypeStruct((groups, length),...  75.8 us
    pallas_call x1, Pallas kernels, finish(): pl.pallas_call(kernel, out_shape=(jax.ShapeDtypeStruct((two, groups * m,...  65.1 us
    unnamed x7, local copies, waits for them, and re-layouts  7.25 us
    another operation x1, other arithmetic, tie_rows(): lax.cummin(jnp.where(next_start == 1, labels[None, :], 127), axis=1, reve...  4.39 us

profile of v7, /device:TPU:1, one launch (start us, length us, event | category | flops | bytes accessed | tf_op | source)
XLA Modules:
  0.0 157.2 jit_solution(6540361709656574074)
XLA Ops:
  0.6 1.0 slice.4
  1.7 0.1 copy.12
  1.8 4.4 %reduce_window_min.10 = s32[256,128]{0,1:T(8,128)S(1)} reduce-window(s32[256,128]{0,1:T(8,128)S(1)} %copy.12, s32[]{:T(128)} %constant.12.clone.1), window={size=1x128 pad=0_0x0_127}, to_apply=%region_1.2 | reduce-window | flops 4161536 | bytes 262148 | tf_op jit(solution)/shard_map/tie_rows/reduce_window_min | solution.py:650
  6.1 0.1 copy.13
  6.2 0.9 iota_select_fusion.1
  7.2 0.1 copy.10
  7.3 0.2 reduce_window_max.10
  7.4 0.1 copy.11
  7.5 1.5 broadcast_bitcast_fusion
  9.0 75.8 %shard_map.67 = (f32[32,32768]{1,0:T(8,128)}, f32[32,32768]{1,0:T(8,128)}, bf16[2,32,32768]{2,1,0:T(8,128)(2,1)}) custom-call(f32[32,32768]{1,0:T(8,128)} %pred_ref.3, s32[32,32768]{1,0:T(8,128)} %ev_ref.1, s32[2048,128]{1,0:T(8,128)} %get-tuple-element.22.first_ref, s32[2048,128]{1,0:T(8,128)} %get-tuple-element.21.last_ref), custom_call_target="tpu_custom_call" | custom-call | tf_op jit(solution)/shard_map/pallas_call | solution.py:614
  84.8 65.1 %shard_map.68 = (bf16[2,128,8192]{2,1,0:T(8,128)(2,1)}, f32[32,64]{1,0:T(8,128)}, f32[32,32768]{1,0:T(8,128)}) custom-call(bf16[2,32,32768]{2,1,0:T(8,128)(2,1)} %get-tuple-element.9.src_ref, s32[32,32768]{1,0:T(8,128)} %leaf_ref.1, f32[32,32768]{1,0:T(8,128)} %get-tuple-element.10.grad_ref, f32[32,32768]{1,0:T(8,128)} %get-tuple-element.11.hess_ref, ...), custom_call_target="tpu_custom_call" | custom-call | tf_op jit(solution)/shard_map/pallas_call | solution.py:398
  149.9 0.0 copy-start.1
  149.9 0.0 copy-start
  150.0 4.6 %copy.18 = f32[32,32768]{1,0:T(8,128)} copy(f32[32,32768]{1,0:T(8,128)} %get-tuple-element.26) | data formatting | bytes 8388608
  154.6 0.0 copy-done.1
  154.6 0.6 copy.19
  155.2 0.0 copy-done
  155.2 2.0 %copy.20 = bf16[2,128,1,8192]{3,1,2,0:T(8,128)(2,1)} copy(bf16[2,128,1,8192]{3,1,2,0:T(8,128)(2,1)S(1)} %bitcast.9) | data formatting | bytes 8388608
  (1 shorter events, 0.0 us)
Async XLA Ops:
  149.9 4.6 %copy-start.1 = (f32[32,64]{1,0:T(8,128)S(1)}, f32[32,64]{1,0:T(8,128)}, u32[]{:S(2)}) copy-start(f32[32,64]{1,0:T(8,128)} %get-tuple-element.27) | copy-start | bytes 24580
  149.9 5.2 %copy-start = (bf16[2,128,8192]{2,1,0:T(8,128)(2,1)S(1)}, bf16[2,128,8192]{2,1,0:T(8,128)(2,1)}, u32[]{:S(2)}) copy-start(bf16[2,128,8192]{2,1,0:T(8,128)(2,1)} %get-tuple-element.14) | copy-start | bytes 12582916

commit v8 on v6

--- a/solution.py
+++ b/solution.py
@@ -557,9 +557,10 @@
                 for k in range(span):
                     risk = one[rows, block_cols(b0 + k)] + later
                     observed = ev_ref[rows, block_cols(b0 + k)].astype(jnp.float32)
-                    inv_one = observed / risk
+                    scale = 1.0 / risk
+                    inv_one = observed * scale
                     firsts.append(inv_one)
-                    seconds.append(inv_one / risk)
+                    seconds.append(inv_one * scale)
                 s = run_sum(jnp.concatenate(firsts + seconds, axis=0), lower)
                 idx = last_ref[pl.ds(pl.multiple_of(b0 * 8, 8), 8 * span), :]
                 idx = jnp.concatenate([idx, idx], axis=0)

time: 154 us -> 154 us (level)
  no operation moved by 1% of the time
where the time goes in v8:
time: 154 us
  Pallas kernels  137 us (89%)
  local copies, waits for them, and re-layouts  10.1 us (7%)
  other arithmetic  5.5 us (4%)
    pallas_call x1, Pallas kernels, front(): pl.pallas_call(kernel, out_shape=(jax.ShapeDtypeStruct((groups, length),...  72.3 us
    pallas_call x1, Pallas kernels, finish(): pl.pallas_call(kernel, out_shape=(jax.ShapeDtypeStruct((two, groups * m,...  65.1 us
    unnamed x7, local copies, waits for them, and re-layouts  7.25 us
    another operation x1, other arithmetic, tie_rows(): lax.cummin(jnp.where(next_start == 1, labels[None, :], 127), axis=1, reve...  4.39 us

profile of v8, /device:TPU:1, one launch (start us, length us, event | category | flops | bytes accessed | tf_op | source)
XLA Modules:
  0.0 153.8 jit_solution(1639595447198413616)
XLA Ops:
  0.6 1.0 slice.4
  1.7 0.1 copy.12
  1.8 4.4 %reduce_window_min.10 = s32[256,128]{0,1:T(8,128)S(1)} reduce-window(s32[256,128]{0,1:T(8,128)S(1)} %copy.12, s32[]{:T(128)} %constant.12.clone.1), window={size=1x128 pad=0_0x0_127}, to_apply=%region_1.2 | reduce-window | flops 4161536 | bytes 262148 | tf_op jit(solution)/shard_map/tie_rows/reduce_window_min | solution.py:652
  6.1 0.1 copy.13
  6.2 0.9 iota_select_fusion.1
  7.2 0.1 copy.10
  7.3 0.2 reduce_window_max.10
  7.4 0.1 copy.11
  7.5 1.5 broadcast_bitcast_fusion
  9.0 72.3 %shard_map.67 = (f32[32,32768]{1,0:T(8,128)}, f32[32,32768]{1,0:T(8,128)}, bf16[2,32,32768]{2,1,0:T(8,128)(2,1)}) custom-call(f32[32,32768]{1,0:T(8,128)} %pred_ref.3, s32[32,32768]{1,0:T(8,128)} %ev_ref.1, s32[2048,128]{1,0:T(8,128)} %get-tuple-element.22.first_ref, s32[2048,128]{1,0:T(8,128)} %get-tuple-element.21.last_ref), custom_call_target="tpu_custom_call" | custom-call | tf_op jit(solution)/shard_map/pallas_call | solution.py:616
  81.3 65.1 %shard_map.68 = (bf16[2,128,8192]{2,1,0:T(8,128)(2,1)}, f32[32,64]{1,0:T(8,128)}, f32[32,32768]{1,0:T(8,128)}) custom-call(bf16[2,32,32768]{2,1,0:T(8,128)(2,1)} %get-tuple-element.9.src_ref, s32[32,32768]{1,0:T(8,128)} %leaf_ref.1, f32[32,32768]{1,0:T(8,128)} %get-tuple-element.10.grad_ref, f32[32,32768]{1,0:T(8,128)} %get-tuple-element.11.hess_ref, ...), custom_call_target="tpu_custom_call" | custom-call | tf_op jit(solution)/shard_map/pallas_call | solution.py:398
  146.5 0.0 copy-start.1
  146.5 0.0 copy-start
  146.5 4.6 %copy.18 = f32[32,32768]{1,0:T(8,128)} copy(f32[32,32768]{1,0:T(8,128)} %get-tuple-element.26) | data formatting | bytes 8388608
  151.1 0.0 copy-done.1
  151.1 0.6 copy.19
  151.8 0.0 copy-done
  151.8 2.0 %copy.20 = bf16[2,128,1,8192]{3,1,2,0:T(8,128)(2,1)} copy(bf16[2,128,1,8192]{3,1,2,0:T(8,128)(2,1)S(1)} %bitcast.9) | data formatting | bytes 8388608
  (1 shorter events, 0.0 us)
Async XLA Ops:
  146.5 4.6 %copy-start.1 = (f32[32,64]{1,0:T(8,128)S(1)}, f32[32,64]{1,0:T(8,128)}, u32[]{:S(2)}) copy-start(f32[32,64]{1,0:T(8,128)} %get-tuple-element.27) | copy-start | bytes 24580
  146.5 5.2 %copy-start = (bf16[2,128,8192]{2,1,0:T(8,128)(2,1)S(1)}, bf16[2,128,8192]{2,1,0:T(8,128)(2,1)}, u32[]{:S(2)}) copy-start(bf16[2,128,8192]{2,1,0:T(8,128)(2,1)} %get-tuple-element.14) | copy-start | bytes 12582916

commit v9 on v8

--- a/solution.py
+++ b/solution.py
@@ -505,11 +505,8 @@
 
         def run_sum(x, matrix):
             hi = x.astype(jnp.bfloat16)
-            rest = x - hi.astype(jnp.float32)
-            mid = rest.astype(jnp.bfloat16)
-            lo = (rest - mid.astype(jnp.float32)).astype(jnp.bfloat16)
+            lo = (x - hi.astype(jnp.float32)).astype(jnp.bfloat16)
             out = jnp.dot(hi, matrix, preferred_element_type=jnp.float32)
-            out = out + jnp.dot(mid, matrix, preferred_element_type=jnp.float32)
             return out + jnp.dot(lo, matrix, preferred_element_type=jnp.float32)
 
         def block_cols(b):

time: 154 us -> 151 us (0.981)
  Pallas kernels: 137 us -> 134 us
    pallas_call x1, Pallas kernels: 72.3 us -> 69.3 us  [front(): pl.pallas_call(kernel, out_shape=(jax.ShapeDtypeStruct((groups, length),...]
where the time goes in v9:
time: 151 us
  Pallas kernels  134 us (89%)
  local copies, waits for them, and re-layouts  10.1 us (7%)
  other arithmetic  5.5 us (4%)
    pallas_call x1, Pallas kernels, front(): pl.pallas_call(kernel, out_shape=(jax.ShapeDtypeStruct((groups, length),...  69.3 us
    pallas_call x1, Pallas kernels, finish(): pl.pallas_call(kernel, out_shape=(jax.ShapeDtypeStruct((two, groups * m,...  65.1 us
    unnamed x7, local copies, waits for them, and re-layouts  7.25 us
    another operation x1, other arithmetic, tie_rows(): lax.cummin(jnp.where(next_start == 1, labels[None, :], 127), axis=1, reve...  4.39 us

profile of v9, /device:TPU:1, one launch (start us, length us, event | category | flops | bytes accessed | tf_op | source)
XLA Modules:
  0.0 150.7 jit_solution(17812620455355799713)
XLA Ops:
  0.6 1.0 slice.4
  1.7 0.1 copy.12
  1.8 4.4 %reduce_window_min.10 = s32[256,128]{0,1:T(8,128)S(1)} reduce-window(s32[256,128]{0,1:T(8,128)S(1)} %copy.12, s32[]{:T(128)} %constant.12.clone.1), window={size=1x128 pad=0_0x0_127}, to_apply=%region_1.2 | reduce-window | flops 4161536 | bytes 262148 | tf_op jit(solution)/shard_map/tie_rows/reduce_window_min | solution.py:649
  6.1 0.1 copy.13
  6.2 0.9 iota_select_fusion.1
  7.2 0.1 copy.10
  7.3 0.2 reduce_window_max.10
  7.4 0.1 copy.11
  7.5 1.5 broadcast_bitcast_fusion
  9.0 69.3 %shard_map.67 = (f32[32,32768]{1,0:T(8,128)}, f32[32,32768]{1,0:T(8,128)}, bf16[2,32,32768]{2,1,0:T(8,128)(2,1)}) custom-call(f32[32,32768]{1,0:T(8,128)} %pred_ref.3, s32[32,32768]{1,0:T(8,128)} %ev_ref.1, s32[2048,128]{1,0:T(8,128)} %get-tuple-element.22.first_ref, s32[2048,128]{1,0:T(8,128)} %get-tuple-element.21.last_ref), custom_call_target="tpu_custom_call" | custom-call | tf_op jit(solution)/shard_map/pallas_call | solution.py:613
  78.3 65.1 %shard_map.68 = (bf16[2,128,8192]{2,1,0:T(8,128)(2,1)}, f32[32,64]{1,0:T(8,128)}, f32[32,32768]{1,0:T(8,128)}) custom-call(bf16[2,32,32768]{2,1,0:T(8,128)(2,1)} %get-tuple-element.9.src_ref, s32[32,32768]{1,0:T(8,128)} %leaf_ref.1, f32[32,32768]{1,0:T(8,128)} %get-tuple-element.10.grad_ref, f32[32,32768]{1,0:T(8,128)} %get-tuple-element.11.hess_ref, ...), custom_call_target="tpu_custom_call" | custom-call | tf_op jit(solution)/shard_map/pallas_call | solution.py:398
  143.4 0.0 copy-start.1
  143.4 0.0 copy-start
  143.4 4.6 %copy.18 = f32[32,32768]{1,0:T(8,128)} copy(f32[32,32768]{1,0:T(8,128)} %get-tuple-element.26) | data formatting | bytes 8388608
  148.1 0.0 copy-done.1
  148.1 0.6 copy.19
  148.7 0.0 copy-done
  148.7 2.0 %copy.20 = bf16[2,128,1,8192]{3,1,2,0:T(8,128)(2,1)} copy(bf16[2,128,1,8192]{3,1,2,0:T(8,128)(2,1)S(1)} %bitcast.9) | data formatting | bytes 8388608
  (1 shorter events, 0.0 us)
Async XLA Ops:
  143.4 4.6 %copy-start.1 = (f32[32,64]{1,0:T(8,128)S(1)}, f32[32,64]{1,0:T(8,128)}, u32[]{:S(2)}) copy-start(f32[32,64]{1,0:T(8,128)} %get-tuple-element.27) | copy-start | bytes 24580
  143.4 5.2 %copy-start = (bf16[2,128,8192]{2,1,0:T(8,128)(2,1)S(1)}, bf16[2,128,8192]{2,1,0:T(8,128)(2,1)}, u32[]{:S(2)}) copy-start(bf16[2,128,8192]{2,1,0:T(8,128)(2,1)} %get-tuple-element.14) | copy-start | bytes 12582916

commit v10 on v9

--- a/solution.py
+++ b/solution.py
@@ -221,7 +221,7 @@
     width = length // m
     tiles = groups // 8
     side = leaves // 8
-    chunk = math.gcd(length, 4096)
+    chunk = math.gcd(length, 8192)
     cols_all = side * 4 * 8
 
     def histogram(leaf_ref, grad_ref, hess_ref, mine):
@@ -375,15 +375,24 @@
             rows = pl.ds(pl.multiple_of(t * 8, 8), 8)
             row = mine[rows, :]
 
+            wide = math.gcd(length, 2048)
+
             def one(step, carry):
-                cols = pl.ds(pl.multiple_of(step * 128, 128), 128)
-                picked = jnp.take_along_axis(
-                    row, leaf_ref[rows, cols], axis=1, mode="promise_in_bounds"
+                cols = pl.ds(pl.multiple_of(step * wide, wide), wide)
+                leaf = leaf_ref[rows, cols]
+                picked = jnp.concatenate(
+                    [
+                        jnp.take_along_axis(
+                            row, leaf[:, k * 128:(k + 1) * 128], axis=1, mode="promise_in_bounds"
+                        )
+                        for k in range(wide // 128)
+                    ],
+                    axis=1,
                 )
                 new_ref[rows, cols] = pred_ref[rows, cols] + picked
                 return carry
 
-            lax.fori_loop(0, length // 128, one, 0, unroll=8)
+            lax.fori_loop(0, length // wide, one, 0)
             return carry
 
         lax.fori_loop(0, tiles, one_tile, 0)

time: 151 us -> 151 us (level)
  no operation moved by 1% of the time
where the time goes in v10:
time: 151 us
  Pallas kernels  134 us (89%)
  local copies, waits for them, and re-layouts  10.1 us (7%)
  other arithmetic  5.5 us (4%)
    pallas_call x1, Pallas kernels, front(): pl.pallas_call(kernel, out_shape=(jax.ShapeDtypeStruct((groups, length),...  69.3 us
    pallas_call x1, Pallas kernels, finish(): pl.pallas_call(kernel, out_shape=(jax.ShapeDtypeStruct((two, groups * m,...  65.1 us
    unnamed x7, local copies, waits for them, and re-layouts  7.25 us
    another operation x1, other arithmetic, tie_rows(): lax.cummin(jnp.where(next_start == 1, labels[None, :], 127), axis=1, reve...  4.39 us

profile of v10, /device:TPU:1, one launch (start us, length us, event | category | flops | bytes accessed | tf_op | source)
XLA Modules:
  0.0 150.7 jit_solution(5392552772042719841)
XLA Ops:
  0.6 1.0 slice.4
  1.7 0.1 copy.12
  1.8 4.4 %reduce_window_min.10 = s32[256,128]{0,1:T(8,128)S(1)} reduce-window(s32[256,128]{0,1:T(8,128)S(1)} %copy.12, s32[]{:T(128)} %constant.12.clone.1), window={size=1x128 pad=0_0x0_127}, to_apply=%region_1.2 | reduce-window | flops 4161536 | bytes 262148 | tf_op jit(solution)/shard_map/tie_rows/reduce_window_min | solution.py:658
  6.1 0.1 copy.13
  6.2 0.9 iota_select_fusion.1
  7.2 0.1 copy.10
  7.3 0.2 reduce_window_max.10
  7.4 0.1 copy.11
  7.5 1.5 broadcast_bitcast_fusion
  9.0 69.3 %shard_map.67 = (f32[32,32768]{1,0:T(8,128)}, f32[32,32768]{1,0:T(8,128)}, bf16[2,32,32768]{2,1,0:T(8,128)(2,1)}) custom-call(f32[32,32768]{1,0:T(8,128)} %pred_ref.3, s32[32,32768]{1,0:T(8,128)} %ev_ref.1, s32[2048,128]{1,0:T(8,128)} %get-tuple-element.22.first_ref, s32[2048,128]{1,0:T(8,128)} %get-tuple-element.21.last_ref), custom_call_target="tpu_custom_call" | custom-call | tf_op jit(solution)/shard_map/pallas_call | solution.py:622
  78.3 65.1 %shard_map.68 = (bf16[2,128,8192]{2,1,0:T(8,128)(2,1)}, f32[32,64]{1,0:T(8,128)}, f32[32,32768]{1,0:T(8,128)}) custom-call(bf16[2,32,32768]{2,1,0:T(8,128)(2,1)} %get-tuple-element.9.src_ref, s32[32,32768]{1,0:T(8,128)} %leaf_ref.1, f32[32,32768]{1,0:T(8,128)} %get-tuple-element.10.grad_ref, f32[32,32768]{1,0:T(8,128)} %get-tuple-element.11.hess_ref, ...), custom_call_target="tpu_custom_call" | custom-call | tf_op jit(solution)/shard_map/pallas_call | solution.py:407
  143.4 0.0 copy-start.1
  143.4 0.0 copy-start
  143.4 4.6 %copy.18 = f32[32,32768]{1,0:T(8,128)} copy(f32[32,32768]{1,0:T(8,128)} %get-tuple-element.26) | data formatting | bytes 8388608
  148.1 0.0 copy-done.1
  148.1 0.6 copy.19
  148.7 0.0 copy-done
  148.7 2.0 %copy.20 = bf16[2,128,1,8192]{3,1,2,0:T(8,128)(2,1)} copy(bf16[2,128,1,8192]{3,1,2,0:T(8,128)(2,1)S(1)} %bitcast.9) | data formatting | bytes 8388608
  (1 shorter events, 0.0 us)
Async XLA Ops:
  143.4 4.6 %copy-start.1 = (f32[32,64]{1,0:T(8,128)S(1)}, f32[32,64]{1,0:T(8,128)}, u32[]{:S(2)}) copy-start(f32[32,64]{1,0:T(8,128)} %get-tuple-element.27) | copy-start | bytes 24580
  143.4 5.2 %copy-start = (bf16[2,128,8192]{2,1,0:T(8,128)(2,1)S(1)}, bf16[2,128,8192]{2,1,0:T(8,128)(2,1)}, u32[]{:S(2)}) copy-start(bf16[2,128,8192]{2,1,0:T(8,128)(2,1)} %get-tuple-element.14) | copy-start | bytes 12582916
